TPU v7x, 128 devices: a whole 4x4x4 slice. The times are simulated.
128 devices in a mesh: lon: 8 (over x_lo, y), lat: 16 (over z, x_hi, core).
Axes of the slice: x: 4 (x_hi: 2, x_lo: 2; x = x_hi * 2 + x_lo), y: 4, z: 4, core: 2. Of those that a mesh axis runs over, the one named last changes fastest.
Arguments:
- velocity: float32 [3, 128, 192, 384], P(None, 'lon', 'lat'), may hold values from -6 to 6
- pressure_in: float32 [128, 192, 384], P('lon', 'lat')
- viscosity: float32 [128, 192, 384], P('lon', 'lat'), as said below
- body_force: float32 [3, 128, 192, 384], P(None, 'lon', 'lat'), may hold values from -60 to 60
- colour_order: int32 [8], replicated, may hold values from 0 to 7, each once
Outputs:
- velocity_out: float32 [3, 128, 192, 384], P(None, 'lon', 'lat')
- pressure_out: float32 [128, 192, 384], P('lon', 'lat')
Inputs may be any that keep to these rules, and one draw needn't show every extreme that they name: colour_order names each of the 8 colours once. viscosity lies between 1 and 1000000.
All inputs are finite; a program needn't handle non-finite values.
Results may differ from a plain program's by a relative error of at most 0.0003.
Values sent between devices are 32-bit elements; how exact they have to be, the bound alone decides.
A program may use at most 320 MiB of HBM per device.

v0:
```python
import math

import jax
import jax.numpy as jnp
from jax import lax
from jax.sharding import PartitionSpec as P

SWEEPS = 2
COLOURS = 8


damping = 0.6
coarse_gain = 0.25
unit_steps = ((1, 0, 0), (0, 1, 0), (0, 0, 1))


def extended_2(block, sides, width, periodic):
    for axis, dim in sides:
        count = lax.axis_size(axis)
        forward = [(i, i + 1) for i in range(count - 1)]
        if periodic:
            forward.append((count - 1, 0))
        backward = [(target, source) for source, target in forward]
        low = lax.ppermute(
            lax.slice_in_dim(block, block.shape[dim] - width, None, axis=dim), axis, forward
        )
        high = lax.ppermute(lax.slice_in_dim(block, 0, width, axis=dim), axis, backward)
        block = jnp.concatenate([low, block, high], axis=dim)
    return block


def stencil_offsets():
    result = []
    for step_x in (-1, 0, 1):
        for step_y in (-1, 0, 1):
            for step_z in (-1, 0, 1):
                reach = abs(step_x) + abs(step_y) + abs(step_z)
                if reach > 0:
                    result.append((step_x, step_y, step_z, 0.5 ** (reach - 1)))
    return result


def slide(values, offset, axis_no):
    if offset == 0:
        return values
    extent = values.shape[axis_no]
    padding = [(0, 0)] * values.ndim
    if offset > 0:
        padding[axis_no] = (0, offset)
        return lax.slice_in_dim(jnp.pad(values, padding), offset, offset + extent, axis=axis_no)
    padding[axis_no] = (-offset, 0)
    return lax.slice_in_dim(jnp.pad(values, padding), 0, extent, axis=axis_no)


def moved(values, step_x, step_y, step_z):
    base = values.ndim - 3
    result = slide(values, step_x, base)
    result = slide(result, step_y, base + 1)
    return slide(result, step_z, base + 2)


def blend(own_value, next_value):
    return 2.0 * own_value * next_value / jnp.maximum(own_value + next_value, 1.0)


def viscous_diagonal(viscous):
    running = jnp.zeros_like(viscous)
    for step_x, step_y, step_z, weight in stencil_offsets():
        running = running + weight * blend(viscous, moved(viscous, step_x, step_y, step_z))
    return running


def residuals(fields, viscous, diagonal, body_force):
    velocity = fields[:3]
    pressure = fields[3]
    applied = diagonal * velocity
    for step_x, step_y, step_z, weight in stencil_offsets():
        coupling = weight * blend(viscous, moved(viscous, step_x, step_y, step_z))
        applied = applied - coupling * moved(velocity, step_x, step_y, step_z)
    gradient = jnp.stack(
        [
            moved(pressure, -unit_step[0], -unit_step[1], -unit_step[2]) - pressure
            for unit_step in unit_steps
        ]
    )
    momentum = body_force - applied - gradient
    continuity = jnp.zeros_like(pressure)
    for axis_no, unit_step in enumerate(unit_steps):
        continuity = continuity - (
            moved(velocity[axis_no], unit_step[0], unit_step[1], unit_step[2]) - velocity[axis_no]
        )
    return (momentum, continuity)


def colour_step(fields, viscous, diagonal, inverse, weight_sum, body_force, chosen):
    momentum, continuity = residuals(fields, viscous, diagonal, body_force)
    scaled = momentum * inverse
    mismatch = -continuity
    for axis_no, unit_step in enumerate(unit_steps):
        mismatch = (
            mismatch
            + moved(scaled[axis_no], unit_step[0], unit_step[1], unit_step[2])
            - scaled[axis_no]
        )
    change = chosen * mismatch / weight_sum
    updates = []
    for axis_no, unit_step in enumerate(unit_steps):
        before = moved(chosen, -unit_step[0], -unit_step[1], -unit_step[2])
        earlier = moved(change, -unit_step[0], -unit_step[1], -unit_step[2])
        updates.append(inverse * ((chosen + before) * momentum[axis_no] + change - earlier))
    velocity = fields[:3] + damping * jnp.stack(updates)
    pressure = fields[3] + damping * change
    return jnp.concatenate([velocity, pressure[None]], axis=0)


def colour_codes(shape):
    lon_parity = jnp.arange(shape[0], dtype=jnp.int32) % 2
    lat_parity = jnp.arange(shape[1], dtype=jnp.int32) % 2
    rad_parity = jnp.arange(shape[2], dtype=jnp.int32) % 2
    return lon_parity[:, None, None] + 2 * lat_parity[None, :, None] + 4 * rad_parity[None, None, :]


def extend(fields, margin):
    beside_all = extended_2(fields, (("lon", 1),), margin, True)
    return extended_2(beside_all, (("lat", 2),), margin, False)


def cycle_kernel(distance, cycle_cells):
    decay_rate = 4.0 / cycle_cells
    screening = 2.0 * math.cosh(decay_rate) - 2.0
    factor = screening / (2.0 * math.sinh(decay_rate) * math.sinh(decay_rate * cycle_cells / 2.0))
    wrapped = jnp.mod(distance, cycle_cells).astype(jnp.float32)
    return factor * jnp.cosh(decay_rate * (cycle_cells / 2.0 - wrapped))


def body(velocity, pressure_in, viscosity, body_force, colour_order):
    groups = 1
    margin = 2 * groups
    lon_cells, lat_cells, rad_cells = viscosity.shape
    lat_total = lax.axis_size("lat") * lat_cells
    lat_global = (
        lax.axis_index("lat") * lat_cells
        - margin
        + jnp.arange(lat_cells + 2 * margin, dtype=jnp.int32)
    )
    inside_lat = ((lat_global >= 0) & (lat_global < lat_total)).astype(jnp.float32)
    inside = jnp.broadcast_to(
        inside_lat[None, :, None], (lon_cells + 2 * margin, lat_cells + 2 * margin, rad_cells)
    )
    constant_fields = jnp.concatenate([body_force, viscosity[None]], axis=0)
    constant_wide = extended_2(constant_fields, (("lon", 1), ("lat", 2)), margin, True) * inside
    force_wide = constant_wide[:3]
    viscous_wide = constant_wide[3]
    diagonal = viscous_diagonal(viscous_wide)
    inverse = jnp.where(inside > 0, 1.0 / jnp.where(diagonal > 0, diagonal, 1.0), 0.0)
    weight_raw = 3.0 * inverse
    for unit_step in unit_steps:
        weight_raw = weight_raw + moved(inverse, unit_step[0], unit_step[1], unit_step[2])
    weight_sum = jnp.where(weight_raw > 0, weight_raw, 1.0)
    parity_code = colour_codes(inside.shape)
    fields = jnp.concatenate([velocity, (pressure_in * viscosity)[None]], axis=0)

    def sweep_block(block_no, current):
        extended = extend(current, margin)
        colour = colour_order[(block_no * groups + 0) % COLOURS]
        chosen = (parity_code == colour).astype(jnp.float32) * inside
        extended = colour_step(
            extended, viscous_wide, diagonal, inverse, weight_sum, force_wide, chosen
        )
        return extended[:, margin : margin + lon_cells, margin : margin + lat_cells, :]

    fields = lax.fori_loop(0, SWEEPS * COLOURS // groups, sweep_block, fields)
    extended = extend(fields, margin)
    momentum, continuity = residuals(extended, viscous_wide, diagonal, force_wide)
    momentum = momentum[:, margin : margin + lon_cells, margin : margin + lat_cells, :]
    lon_coarse = lon_cells // 8
    lat_coarse = lat_cells // 4
    rad_coarse = rad_cells // 4
    cycle_cells = lax.axis_size("lon") * lon_coarse
    own_first = lax.axis_index("lon") * lon_coarse
    summed = momentum.reshape(3, lon_coarse, 8, lat_coarse, 4, rad_coarse, 4).sum(axis=(2, 4, 6))
    viscous_sum = viscosity.reshape(lon_coarse, 8, lat_coarse, 4, rad_coarse, 4).sum(axis=(1, 3, 5))
    coarse = jnp.transpose(summed / viscous_sum[None], (1, 0, 2, 3))
    shard_piece = lax.all_gather(coarse, "lon", axis=0, tiled=True)
    sources = jnp.arange(shard_piece.shape[0], dtype=jnp.int32)
    targets = own_first + jnp.arange(lon_coarse, dtype=jnp.int32)
    kernel_table = cycle_kernel(targets[None, :] - sources[:, None], cycle_cells)
    smooth = jnp.einsum("jcyz,ji->icyz", shard_piece, kernel_table, precision=lax.Precision.HIGHEST)
    smooth = jnp.transpose(smooth, (1, 0, 2, 3))
    spread = jnp.repeat(jnp.repeat(jnp.repeat(smooth, 8, axis=1), 4, axis=2), 4, axis=3)
    velocity_out = fields[:3] + coarse_gain * spread
    pressure_out = fields[3] / viscosity
    return (velocity_out, pressure_out)


def solution(mesh):
    placed = (
        P(None, "lon", "lat", None),
        P("lon", "lat", None),
        P("lon", "lat", None),
        P(None, "lon", "lat", None),
        P(),
    )
    return jax.shard_map(
        body,
        mesh=mesh,
        in_specs=placed,
        out_specs=(P(None, "lon", "lat", None), P("lon", "lat", None)),
        check_vma=False,
    )
```

profile of v0, /device:TPU:1, one launch (start us, length us, event | category | flops | bytes accessed | tf_op | source)
XLA Modules:
  0.0 925.8 jit_solution(6954030963657207484)
XLA Ops:
  21.4 4.7 collective-permute-done.7
  29.6 6.9 fusion.140
  37.5 738.2 %while.16 = (s32[]{:T(128)}, f32[4,16,12,384]{3,2,1,0:T(8,128)S(1)}, s32[8]{0:T(128)}, f32[20,16,384]{2,1,0:T(8,128)}, f32[20,16,384]{2,1,0:T(8,128)S(1)}, /*ind...) while((s32[]{:T(128)}, ...), condition=%wide.region_1.2_spmd.clone, body=%wide.region_0.1_spmd.clone.sunk | while | flops 44777472 | bytes 127703776 | solution.py:172
  53.8 5.1 collective-permute-start.3
  66.9 10.8 %broadcast_multiply_fusion.4 = (f32[3,20,16,384]{3,2,1,0:T(8,128)S(1)}, f32[3,20,16,384]{3,2,1,0:T(8,128)S(1)}) fusion(f32[20,16,384]{2,1,0:T(8,128)S(1)} %get-tuple-element.668, f32[1,20,16,384]{3,2,1,0:T(8,128)} %get-tuple-element.575, f32[1,20,16,384]{3,2,1,0:T(8,128)} %get-tuple-element.576, f32[1,20,16,384]{3,2,1,0:T(8,128)} %get-tuple-element.577, ...), kind=kLoop, calls=%fused_computation.81.clone.1 | loop fusion | flops 21381120 | bytes 32931840 | tf_op jit(solution)/shard_map/while/body/eval_jaxpr/mul | solution.py:97
  98.3 6.5 collective-permute-start.3
  112.7 10.8 %broadcast_multiply_fusion.4 = (f32[3,20,16,384]{3,2,1,0:T(8,128)S(1)}, f32[3,20,16,384]{3,2,1,0:T(8,128)S(1)}) fusion(f32[20,16,384]{2,1,0:T(8,128)S(1)} %get-tuple-element.668, f32[1,20,16,384]{3,2,1,0:T(8,128)} %get-tuple-element.575, f32[1,20,16,384]{3,2,1,0:T(8,128)} %get-tuple-element.576, f32[1,20,16,384]{3,2,1,0:T(8,128)} %get-tuple-element.577, ...), kind=kLoop, calls=%fused_computation.81.clone.1 | loop fusion | flops 21381120 | bytes 32931840 | tf_op jit(solution)/shard_map/while/body/eval_jaxpr/mul | solution.py:97
  144.2 6.5 collective-permute-start.3
  158.6 10.8 %broadcast_multiply_fusion.4 = (f32[3,20,16,384]{3,2,1,0:T(8,128)S(1)}, f32[3,20,16,384]{3,2,1,0:T(8,128)S(1)}) fusion(f32[20,16,384]{2,1,0:T(8,128)S(1)} %get-tuple-element.668, f32[1,20,16,384]{3,2,1,0:T(8,128)} %get-tuple-element.575, f32[1,20,16,384]{3,2,1,0:T(8,128)} %get-tuple-element.576, f32[1,20,16,384]{3,2,1,0:T(8,128)} %get-tuple-element.577, ...), kind=kLoop, calls=%fused_computation.81.clone.1 | loop fusion | flops 21381120 | bytes 32931840 | tf_op jit(solution)/shard_map/while/body/eval_jaxpr/mul | solution.py:97
  190.0 6.5 collective-permute-start.3
  204.4 10.8 %broadcast_multiply_fusion.4 = (f32[3,20,16,384]{3,2,1,0:T(8,128)S(1)}, f32[3,20,16,384]{3,2,1,0:T(8,128)S(1)}) fusion(f32[20,16,384]{2,1,0:T(8,128)S(1)} %get-tuple-element.668, f32[1,20,16,384]{3,2,1,0:T(8,128)} %get-tuple-element.575, f32[1,20,16,384]{3,2,1,0:T(8,128)} %get-tuple-element.576, f32[1,20,16,384]{3,2,1,0:T(8,128)} %get-tuple-element.577, ...), kind=kLoop, calls=%fused_computation.81.clone.1 | loop fusion | flops 21381120 | bytes 32931840 | tf_op jit(solution)/shard_map/while/body/eval_jaxpr/mul | solution.py:97
  235.9 6.5 collective-permute-start.3
  250.3 10.8 %broadcast_multiply_fusion.4 = (f32[3,20,16,384]{3,2,1,0:T(8,128)S(1)}, f32[3,20,16,384]{3,2,1,0:T(8,128)S(1)}) fusion(f32[20,16,384]{2,1,0:T(8,128)S(1)} %get-tuple-element.668, f32[1,20,16,384]{3,2,1,0:T(8,128)} %get-tuple-element.575, f32[1,20,16,384]{3,2,1,0:T(8,128)} %get-tuple-element.576, f32[1,20,16,384]{3,2,1,0:T(8,128)} %get-tuple-element.577, ...), kind=kLoop, calls=%fused_computation.81.clone.1 | loop fusion | flops 21381120 | bytes 32931840 | tf_op jit(solution)/shard_map/while/body/eval_jaxpr/mul | solution.py:97
  281.7 6.5 collective-permute-start.3
  296.1 10.8 %broadcast_multiply_fusion.4 = (f32[3,20,16,384]{3,2,1,0:T(8,128)S(1)}, f32[3,20,16,384]{3,2,1,0:T(8,128)S(1)}) fusion(f32[20,16,384]{2,1,0:T(8,128)S(1)} %get-tuple-element.668, f32[1,20,16,384]{3,2,1,0:T(8,128)} %get-tuple-element.575, f32[1,20,16,384]{3,2,1,0:T(8,128)} %get-tuple-element.576, f32[1,20,16,384]{3,2,1,0:T(8,128)} %get-tuple-element.577, ...), kind=kLoop, calls=%fused_computation.81.clone.1 | loop fusion | flops 21381120 | bytes 32931840 | tf_op jit(solution)/shard_map/while/body/eval_jaxpr/mul | solution.py:97
  327.5 6.5 collective-permute-start.3
  341.9 10.8 %broadcast_multiply_fusion.4 = (f32[3,20,16,384]{3,2,1,0:T(8,128)S(1)}, f32[3,20,16,384]{3,2,1,0:T(8,128)S(1)}) fusion(f32[20,16,384]{2,1,0:T(8,128)S(1)} %get-tuple-element.668, f32[1,20,16,384]{3,2,1,0:T(8,128)} %get-tuple-element.575, f32[1,20,16,384]{3,2,1,0:T(8,128)} %get-tuple-element.576, f32[1,20,16,384]{3,2,1,0:T(8,128)} %get-tuple-element.577, ...), kind=kLoop, calls=%fused_computation.81.clone.1 | loop fusion | flops 21381120 | bytes 32931840 | tf_op jit(solution)/shard_map/while/body/eval_jaxpr/mul | solution.py:97
  373.4 6.5 collective-permute-start.3
  387.8 10.8 %broadcast_multiply_fusion.4 = (f32[3,20,16,384]{3,2,1,0:T(8,128)S(1)}, f32[3,20,16,384]{3,2,1,0:T(8,128)S(1)}) fusion(f32[20,16,384]{2,1,0:T(8,128)S(1)} %get-tuple-element.668, f32[1,20,16,384]{3,2,1,0:T(8,128)} %get-tuple-element.575, f32[1,20,16,384]{3,2,1,0:T(8,128)} %get-tuple-element.576, f32[1,20,16,384]{3,2,1,0:T(8,128)} %get-tuple-element.577, ...), kind=kLoop, calls=%fused_computation.81.clone.1 | loop fusion | flops 21381120 | bytes 32931840 | tf_op jit(solution)/shard_map/while/body/eval_jaxpr/mul | solution.py:97
  419.2 6.5 collective-permute-start.3
  433.6 10.8 %broadcast_multiply_fusion.4 = (f32[3,20,16,384]{3,2,1,0:T(8,128)S(1)}, f32[3,20,16,384]{3,2,1,0:T(8,128)S(1)}) fusion(f32[20,16,384]{2,1,0:T(8,128)S(1)} %get-tuple-element.668, f32[1,20,16,384]{3,2,1,0:T(8,128)} %get-tuple-element.575, f32[1,20,16,384]{3,2,1,0:T(8,128)} %get-tuple-element.576, f32[1,20,16,384]{3,2,1,0:T(8,128)} %get-tuple-element.577, ...), kind=kLoop, calls=%fused_computation.81.clone.1 | loop fusion | flops 21381120 | bytes 32931840 | tf_op jit(solution)/shard_map/while/body/eval_jaxpr/mul | solution.py:97
  465.1 6.9 collective-permute-start.3
  480.0 10.8 %broadcast_multiply_fusion.4 = (f32[3,20,16,384]{3,2,1,0:T(8,128)S(1)}, f32[3,20,16,384]{3,2,1,0:T(8,128)S(1)}) fusion(f32[20,16,384]{2,1,0:T(8,128)S(1)} %get-tuple-element.668, f32[1,20,16,384]{3,2,1,0:T(8,128)} %get-tuple-element.575, f32[1,20,16,384]{3,2,1,0:T(8,128)} %get-tuple-element.576, f32[1,20,16,384]{3,2,1,0:T(8,128)} %get-tuple-element.577, ...), kind=kLoop, calls=%fused_computation.81.clone.1 | loop fusion | flops 21381120 | bytes 32931840 | tf_op jit(solution)/shard_map/while/body/eval_jaxpr/mul | solution.py:97
  511.4 7.4 collective-permute-start.3
  526.7 10.8 %broadcast_multiply_fusion.4 = (f32[3,20,16,384]{3,2,1,0:T(8,128)S(1)}, f32[3,20,16,384]{3,2,1,0:T(8,128)S(1)}) fusion(f32[20,16,384]{2,1,0:T(8,128)S(1)} %get-tuple-element.668, f32[1,20,16,384]{3,2,1,0:T(8,128)} %get-tuple-element.575, f32[1,20,16,384]{3,2,1,0:T(8,128)} %get-tuple-element.576, f32[1,20,16,384]{3,2,1,0:T(8,128)} %get-tuple-element.577, ...), kind=kLoop, calls=%fused_computation.81.clone.1 | loop fusion | flops 21381120 | bytes 32931840 | tf_op jit(solution)/shard_map/while/body/eval_jaxpr/mul | solution.py:97
  558.1 7.4 collective-permute-start.3
  573.5 10.8 %broadcast_multiply_fusion.4 = (f32[3,20,16,384]{3,2,1,0:T(8,128)S(1)}, f32[3,20,16,384]{3,2,1,0:T(8,128)S(1)}) fusion(f32[20,16,384]{2,1,0:T(8,128)S(1)} %get-tuple-element.668, f32[1,20,16,384]{3,2,1,0:T(8,128)} %get-tuple-element.575, f32[1,20,16,384]{3,2,1,0:T(8,128)} %get-tuple-element.576, f32[1,20,16,384]{3,2,1,0:T(8,128)} %get-tuple-element.577, ...), kind=kLoop, calls=%fused_computation.81.clone.1 | loop fusion | flops 21381120 | bytes 32931840 | tf_op jit(solution)/shard_map/while/body/eval_jaxpr/mul | solution.py:97
  604.9 7.4 collective-permute-start.3
  620.2 10.8 %broadcast_multiply_fusion.4 = (f32[3,20,16,384]{3,2,1,0:T(8,128)S(1)}, f32[3,20,16,384]{3,2,1,0:T(8,128)S(1)}) fusion(f32[20,16,384]{2,1,0:T(8,128)S(1)} %get-tuple-element.668, f32[1,20,16,384]{3,2,1,0:T(8,128)} %get-tuple-element.575, f32[1,20,16,384]{3,2,1,0:T(8,128)} %get-tuple-element.576, f32[1,20,16,384]{3,2,1,0:T(8,128)} %get-tuple-element.577, ...), kind=kLoop, calls=%fused_computation.81.clone.1 | loop fusion | flops 21381120 | bytes 32931840 | tf_op jit(solution)/shard_map/while/body/eval_jaxpr/mul | solution.py:97
  651.6 7.4 collective-permute-start.3
  666.9 10.8 %broadcast_multiply_fusion.4 = (f32[3,20,16,384]{3,2,1,0:T(8,128)S(1)}, f32[3,20,16,384]{3,2,1,0:T(8,128)S(1)}) fusion(f32[20,16,384]{2,1,0:T(8,128)S(1)} %get-tuple-element.668, f32[1,20,16,384]{3,2,1,0:T(8,128)} %get-tuple-element.575, f32[1,20,16,384]{3,2,1,0:T(8,128)} %get-tuple-element.576, f32[1,20,16,384]{3,2,1,0:T(8,128)} %get-tuple-element.577, ...), kind=kLoop, calls=%fused_computation.81.clone.1 | loop fusion | flops 21381120 | bytes 32931840 | tf_op jit(solution)/shard_map/while/body/eval_jaxpr/mul | solution.py:97
  698.4 7.4 collective-permute-start.3
  713.7 10.8 %broadcast_multiply_fusion.4 = (f32[3,20,16,384]{3,2,1,0:T(8,128)S(1)}, f32[3,20,16,384]{3,2,1,0:T(8,128)S(1)}) fusion(f32[20,16,384]{2,1,0:T(8,128)S(1)} %get-tuple-element.668, f32[1,20,16,384]{3,2,1,0:T(8,128)} %get-tuple-element.575, f32[1,20,16,384]{3,2,1,0:T(8,128)} %get-tuple-element.576, f32[1,20,16,384]{3,2,1,0:T(8,128)} %get-tuple-element.577, ...), kind=kLoop, calls=%fused_computation.81.clone.1 | loop fusion | flops 21381120 | bytes 32931840 | tf_op jit(solution)/shard_map/while/body/eval_jaxpr/mul | solution.py:97
  745.1 7.4 collective-permute-start.3
  760.4 10.8 %broadcast_multiply_fusion.4 = (f32[3,20,16,384]{3,2,1,0:T(8,128)S(1)}, f32[3,20,16,384]{3,2,1,0:T(8,128)S(1)}) fusion(f32[20,16,384]{2,1,0:T(8,128)S(1)} %get-tuple-element.668, f32[1,20,16,384]{3,2,1,0:T(8,128)} %get-tuple-element.575, f32[1,20,16,384]{3,2,1,0:T(8,128)} %get-tuple-element.576, f32[1,20,16,384]{3,2,1,0:T(8,128)} %get-tuple-element.577, ...), kind=kLoop, calls=%fused_computation.81.clone.1 | loop fusion | flops 21381120 | bytes 32931840 | tf_op jit(solution)/shard_map/while/body/eval_jaxpr/mul | solution.py:97
  779.1 5.8 reshape.151
  784.9 4.9 reduce_sum.19
  798.3 5.2 copy.58
  803.9 7.4 collective-permute-start.10
  814.9 8.2 collective-permute-done.11
  834.7 17.9 %fusion.109 = f32[3,20,16,384]{3,2,1,0:T(8,128)} fusion(f32[3,20,16,384]{3,2,1,0:T(8,128)} %get-tuple-element.425, f32[3,20,16,384]{3,2,1,0:T(8,128)} %copy-done.11, f32[3,20,16,384]{3,2,1,0:T(8,128)} %get-tuple-element.424, f32[3,20,16,384]{3,2,1,0:T(8,128)} %get-tuple-element.422, f32[3,20,16,384]{3,2,1,0:T(8,128)} %copy-done.9, ...), kind=kLoop, calls=%fused_computation.253 | loop fusion | flops 16588800 | bytes 24576000 | tf_op jit(solution)/shard_map/sub | solution.py:79
  852.5 5.3 fusion.125
  857.8 5.2 copy.53
  863.0 14.3 %reshape.150 = f32[3,2,8,3,4,96,4]{2,1,6,5,4,3,0:T(2,128)} reshape(f32[3,16,12,384]{1,3,2,0:T(8,128)} %copy.53) | data formatting | bytes 1769472 | tf_op jit(solution)/shard_map/reshape | solution.py:181
  877.4 11.6 %reduce_sum.18 = f32[3,2,3,96]{1,3,2,0:T(8,128)S(1)} reduce(f32[3,2,8,3,4,96,4]{2,1,6,5,4,3,0:T(2,128)} %reshape.150, f32[]{:T(128)} %constant.185.clone.1), dimensions={2,4,6}, to_apply=%region_2.3 | reduce | flops 219456 | bytes 891652 | tf_op jit(solution)/shard_map/reduce_sum | solution.py:181
  889.2 22.2 %all_gather.3 = f32[16,3,3,96]{3,2,1,0:T(4,128)S(1)} all-gather(f32[2,3,3,96]{3,2,1,0:T(4,128)S(1)} %copy.55), channel_id=1, replica_groups=mesh['lon'=8,'lat'=16] {'lon'}, dimensions={0}, use_global_device_ids=true | all-gather | bytes 62208 | tf_op jit(solution)/shard_map/all_gather | solution.py:184
  913.3 6.9 add.1008
  920.2 5.6 copy.60
  (789 shorter events, 508.9 us)
Async XLA Ops:
  38.3 11.4 %collective-permute-start = (f32[4,2,12,384]{3,2,1,0:T(8,128)}, f32[4,2,12,384]{3,2,1,0:T(8,128)}, u32[]{:S(2)}, u32[]{:S(2)}) collective-permute-start(f32[4,2,12,384]{3,2,1,0:T(8,128)} %get-tuple-element.570), channel_id=1, source_target_pairs={{0,16},{16,32},{32,48},{48,64},{64,80},{80,96},{96,112},{112,0},{1... | collective-permute-start | bytes 442376 | tf_op jit(solution)/shard_map/while/body/eval_jaxpr/ppermute | solution.py:24
  38.8 12.0 %collective-permute-start.1 = (f32[4,2,12,384]{3,2,1,0:T(8,128)}, f32[4,2,12,384]{3,2,1,0:T(8,128)}, u32[]{:S(2)}, u32[]{:S(2)}) collective-permute-start(f32[4,2,12,384]{3,2,1,0:T(8,128)} %get-tuple-element.571), channel_id=1, source_target_pairs={{16,0},{32,16},{48,32},{64,48},{80,64},{96,80},{112,96},{0,112},{1... | collective-permute-start | bytes 442376 | tf_op jit(solution)/shard_map/while/body/eval_jaxpr/ppermute | solution.py:27
  82.9 11.3 %collective-permute-start = (f32[4,2,12,384]{3,2,1,0:T(8,128)}, f32[4,2,12,384]{3,2,1,0:T(8,128)}, u32[]{:S(2)}, u32[]{:S(2)}) collective-permute-start(f32[4,2,12,384]{3,2,1,0:T(8,128)} %get-tuple-element.570), channel_id=1, source_target_pairs={{0,16},{16,32},{32,48},{48,64},{64,80},{80,96},{96,112},{112,0},{1... | collective-permute-start | bytes 442376 | tf_op jit(solution)/shard_map/while/body/eval_jaxpr/ppermute | solution.py:24
  82.9 12.4 %collective-permute-start.1 = (f32[4,2,12,384]{3,2,1,0:T(8,128)}, f32[4,2,12,384]{3,2,1,0:T(8,128)}, u32[]{:S(2)}, u32[]{:S(2)}) collective-permute-start(f32[4,2,12,384]{3,2,1,0:T(8,128)} %get-tuple-element.571), channel_id=1, source_target_pairs={{16,0},{32,16},{48,32},{64,48},{80,64},{96,80},{112,96},{0,112},{1... | collective-permute-start | bytes 442376 | tf_op jit(solution)/shard_map/while/body/eval_jaxpr/ppermute | solution.py:27
  128.8 11.3 %collective-permute-start = (f32[4,2,12,384]{3,2,1,0:T(8,128)}, f32[4,2,12,384]{3,2,1,0:T(8,128)}, u32[]{:S(2)}, u32[]{:S(2)}) collective-permute-start(f32[4,2,12,384]{3,2,1,0:T(8,128)} %get-tuple-element.570), channel_id=1, source_target_pairs={{0,16},{16,32},{32,48},{48,64},{64,80},{80,96},{96,112},{112,0},{1... | collective-permute-start | bytes 442376 | tf_op jit(solution)/shard_map/while/body/eval_jaxpr/ppermute | solution.py:24
  128.8 12.4 %collective-permute-start.1 = (f32[4,2,12,384]{3,2,1,0:T(8,128)}, f32[4,2,12,384]{3,2,1,0:T(8,128)}, u32[]{:S(2)}, u32[]{:S(2)}) collective-permute-start(f32[4,2,12,384]{3,2,1,0:T(8,128)} %get-tuple-element.571), channel_id=1, source_target_pairs={{16,0},{32,16},{48,32},{64,48},{80,64},{96,80},{112,96},{0,112},{1... | collective-permute-start | bytes 442376 | tf_op jit(solution)/shard_map/while/body/eval_jaxpr/ppermute | solution.py:27
  174.6 11.3 %collective-permute-start = (f32[4,2,12,384]{3,2,1,0:T(8,128)}, f32[4,2,12,384]{3,2,1,0:T(8,128)}, u32[]{:S(2)}, u32[]{:S(2)}) collective-permute-start(f32[4,2,12,384]{3,2,1,0:T(8,128)} %get-tuple-element.570), channel_id=1, source_target_pairs={{0,16},{16,32},{32,48},{48,64},{64,80},{80,96},{96,112},{112,0},{1... | collective-permute-start | bytes 442376 | tf_op jit(solution)/shard_map/while/body/eval_jaxpr/ppermute | solution.py:24
  174.6 12.4 %collective-permute-start.1 = (f32[4,2,12,384]{3,2,1,0:T(8,128)}, f32[4,2,12,384]{3,2,1,0:T(8,128)}, u32[]{:S(2)}, u32[]{:S(2)}) collective-permute-start(f32[4,2,12,384]{3,2,1,0:T(8,128)} %get-tuple-element.571), channel_id=1, source_target_pairs={{16,0},{32,16},{48,32},{64,48},{80,64},{96,80},{112,96},{0,112},{1... | collective-permute-start | bytes 442376 | tf_op jit(solution)/shard_map/while/body/eval_jaxpr/ppermute | solution.py:27
  220.4 11.3 %collective-permute-start = (f32[4,2,12,384]{3,2,1,0:T(8,128)}, f32[4,2,12,384]{3,2,1,0:T(8,128)}, u32[]{:S(2)}, u32[]{:S(2)}) collective-permute-start(f32[4,2,12,384]{3,2,1,0:T(8,128)} %get-tuple-element.570), channel_id=1, source_target_pairs={{0,16},{16,32},{32,48},{48,64},{64,80},{80,96},{96,112},{112,0},{1... | collective-permute-start | bytes 442376 | tf_op jit(solution)/shard_map/while/body/eval_jaxpr/ppermute | solution.py:24
  220.4 12.4 %collective-permute-start.1 = (f32[4,2,12,384]{3,2,1,0:T(8,128)}, f32[4,2,12,384]{3,2,1,0:T(8,128)}, u32[]{:S(2)}, u32[]{:S(2)}) collective-permute-start(f32[4,2,12,384]{3,2,1,0:T(8,128)} %get-tuple-element.571), channel_id=1, source_target_pairs={{16,0},{32,16},{48,32},{64,48},{80,64},{96,80},{112,96},{0,112},{1... | collective-permute-start | bytes 442376 | tf_op jit(solution)/shard_map/while/body/eval_jaxpr/ppermute | solution.py:27
  266.3 11.3 %collective-permute-start = (f32[4,2,12,384]{3,2,1,0:T(8,128)}, f32[4,2,12,384]{3,2,1,0:T(8,128)}, u32[]{:S(2)}, u32[]{:S(2)}) collective-permute-start(f32[4,2,12,384]{3,2,1,0:T(8,128)} %get-tuple-element.570), channel_id=1, source_target_pairs={{0,16},{16,32},{32,48},{48,64},{64,80},{80,96},{96,112},{112,0},{1... | collective-permute-start | bytes 442376 | tf_op jit(solution)/shard_map/while/body/eval_jaxpr/ppermute | solution.py:24
  266.3 12.4 %collective-permute-start.1 = (f32[4,2,12,384]{3,2,1,0:T(8,128)}, f32[4,2,12,384]{3,2,1,0:T(8,128)}, u32[]{:S(2)}, u32[]{:S(2)}) collective-permute-start(f32[4,2,12,384]{3,2,1,0:T(8,128)} %get-tuple-element.571), channel_id=1, source_target_pairs={{16,0},{32,16},{48,32},{64,48},{80,64},{96,80},{112,96},{0,112},{1... | collective-permute-start | bytes 442376 | tf_op jit(solution)/shard_map/while/body/eval_jaxpr/ppermute | solution.py:27
  312.1 11.3 %collective-permute-start = (f32[4,2,12,384]{3,2,1,0:T(8,128)}, f32[4,2,12,384]{3,2,1,0:T(8,128)}, u32[]{:S(2)}, u32[]{:S(2)}) collective-permute-start(f32[4,2,12,384]{3,2,1,0:T(8,128)} %get-tuple-element.570), channel_id=1, source_target_pairs={{0,16},{16,32},{32,48},{48,64},{64,80},{80,96},{96,112},{112,0},{1... | collective-permute-start | bytes 442376 | tf_op jit(solution)/shard_map/while/body/eval_jaxpr/ppermute | solution.py:24
  312.1 12.4 %collective-permute-start.1 = (f32[4,2,12,384]{3,2,1,0:T(8,128)}, f32[4,2,12,384]{3,2,1,0:T(8,128)}, u32[]{:S(2)}, u32[]{:S(2)}) collective-permute-start(f32[4,2,12,384]{3,2,1,0:T(8,128)} %get-tuple-element.571), channel_id=1, source_target_pairs={{16,0},{32,16},{48,32},{64,48},{80,64},{96,80},{112,96},{0,112},{1... | collective-permute-start | bytes 442376 | tf_op jit(solution)/shard_map/while/body/eval_jaxpr/ppermute | solution.py:27
  358.0 11.3 %collective-permute-start = (f32[4,2,12,384]{3,2,1,0:T(8,128)}, f32[4,2,12,384]{3,2,1,0:T(8,128)}, u32[]{:S(2)}, u32[]{:S(2)}) collective-permute-start(f32[4,2,12,384]{3,2,1,0:T(8,128)} %get-tuple-element.570), channel_id=1, source_target_pairs={{0,16},{16,32},{32,48},{48,64},{64,80},{80,96},{96,112},{112,0},{1... | collective-permute-start | bytes 442376 | tf_op jit(solution)/shard_map/while/body/eval_jaxpr/ppermute | solution.py:24
  358.0 12.4 %collective-permute-start.1 = (f32[4,2,12,384]{3,2,1,0:T(8,128)}, f32[4,2,12,384]{3,2,1,0:T(8,128)}, u32[]{:S(2)}, u32[]{:S(2)}) collective-permute-start(f32[4,2,12,384]{3,2,1,0:T(8,128)} %get-tuple-element.571), channel_id=1, source_target_pairs={{16,0},{32,16},{48,32},{64,48},{80,64},{96,80},{112,96},{0,112},{1... | collective-permute-start | bytes 442376 | tf_op jit(solution)/shard_map/while/body/eval_jaxpr/ppermute | solution.py:27
  403.8 11.3 %collective-permute-start = (f32[4,2,12,384]{3,2,1,0:T(8,128)}, f32[4,2,12,384]{3,2,1,0:T(8,128)}, u32[]{:S(2)}, u32[]{:S(2)}) collective-permute-start(f32[4,2,12,384]{3,2,1,0:T(8,128)} %get-tuple-element.570), channel_id=1, source_target_pairs={{0,16},{16,32},{32,48},{48,64},{64,80},{80,96},{96,112},{112,0},{1... | collective-permute-start | bytes 442376 | tf_op jit(solution)/shard_map/while/body/eval_jaxpr/ppermute | solution.py:24
  403.8 12.4 %collective-permute-start.1 = (f32[4,2,12,384]{3,2,1,0:T(8,128)}, f32[4,2,12,384]{3,2,1,0:T(8,128)}, u32[]{:S(2)}, u32[]{:S(2)}) collective-permute-start(f32[4,2,12,384]{3,2,1,0:T(8,128)} %get-tuple-element.571), channel_id=1, source_target_pairs={{16,0},{32,16},{48,32},{64,48},{80,64},{96,80},{112,96},{0,112},{1... | collective-permute-start | bytes 442376 | tf_op jit(solution)/shard_map/while/body/eval_jaxpr/ppermute | solution.py:27
  449.7 11.3 %collective-permute-start = (f32[4,2,12,384]{3,2,1,0:T(8,128)}, f32[4,2,12,384]{3,2,1,0:T(8,128)}, u32[]{:S(2)}, u32[]{:S(2)}) collective-permute-start(f32[4,2,12,384]{3,2,1,0:T(8,128)} %get-tuple-element.570), channel_id=1, source_target_pairs={{0,16},{16,32},{32,48},{48,64},{64,80},{80,96},{96,112},{112,0},{1... | collective-permute-start | bytes 442376 | tf_op jit(solution)/shard_map/while/body/eval_jaxpr/ppermute | solution.py:24
  449.7 12.4 %collective-permute-start.1 = (f32[4,2,12,384]{3,2,1,0:T(8,128)}, f32[4,2,12,384]{3,2,1,0:T(8,128)}, u32[]{:S(2)}, u32[]{:S(2)}) collective-permute-start(f32[4,2,12,384]{3,2,1,0:T(8,128)} %get-tuple-element.571), channel_id=1, source_target_pairs={{16,0},{32,16},{48,32},{64,48},{80,64},{96,80},{112,96},{0,112},{1... | collective-permute-start | bytes 442376 | tf_op jit(solution)/shard_map/while/body/eval_jaxpr/ppermute | solution.py:27
  463.2 10.8 %collective-permute-start.2 = (f32[4,20,2,384]{3,2,1,0:T(2,128)S(1)}, f32[4,20,2,384]{3,2,1,0:T(2,128)S(1)}, u32[]{:S(2)}, u32[]{:S(2)}) collective-permute-start(f32[4,20,2,384]{3,2,1,0:T(2,128)S(1)} %get-tuple-element.572), channel_id=1, source_target_pairs={{1,0},{2,1},{3,2},{4,3},{5,4},{6,5},{7,6},{8,7},{9,8},{10,9},{11,1... | collective-permute-start | bytes 737288 | tf_op jit(solution)/shard_map/while/body/eval_jaxpr/ppermute | solution.py:27
  496.0 11.3 %collective-permute-start = (f32[4,2,12,384]{3,2,1,0:T(8,128)}, f32[4,2,12,384]{3,2,1,0:T(8,128)}, u32[]{:S(2)}, u32[]{:S(2)}) collective-permute-start(f32[4,2,12,384]{3,2,1,0:T(8,128)} %get-tuple-element.570), channel_id=1, source_target_pairs={{0,16},{16,32},{32,48},{48,64},{64,80},{80,96},{96,112},{112,0},{1... | collective-permute-start | bytes 442376 | tf_op jit(solution)/shard_map/while/body/eval_jaxpr/ppermute | solution.py:24
  496.0 12.4 %collective-permute-start.1 = (f32[4,2,12,384]{3,2,1,0:T(8,128)}, f32[4,2,12,384]{3,2,1,0:T(8,128)}, u32[]{:S(2)}, u32[]{:S(2)}) collective-permute-start(f32[4,2,12,384]{3,2,1,0:T(8,128)} %get-tuple-element.571), channel_id=1, source_target_pairs={{16,0},{32,16},{48,32},{64,48},{80,64},{96,80},{112,96},{0,112},{1... | collective-permute-start | bytes 442376 | tf_op jit(solution)/shard_map/while/body/eval_jaxpr/ppermute | solution.py:27
  509.5 11.2 %collective-permute-start.2 = (f32[4,20,2,384]{3,2,1,0:T(2,128)S(1)}, f32[4,20,2,384]{3,2,1,0:T(2,128)S(1)}, u32[]{:S(2)}, u32[]{:S(2)}) collective-permute-start(f32[4,20,2,384]{3,2,1,0:T(2,128)S(1)} %get-tuple-element.572), channel_id=1, source_target_pairs={{1,0},{2,1},{3,2},{4,3},{5,4},{6,5},{7,6},{8,7},{9,8},{10,9},{11,1... | collective-permute-start | bytes 737288 | tf_op jit(solution)/shard_map/while/body/eval_jaxpr/ppermute | solution.py:27
  511.4 10.5 %collective-permute-start.3 = (f32[4,20,2,384]{3,2,1,0:T(2,128)S(1)}, f32[4,20,2,384]{3,2,1,0:T(2,128)S(1)}, u32[]{:S(2)}, u32[]{:S(2)}) collective-permute-start(f32[4,20,2,384]{3,2,1,0:T(2,128)S(1)} %get-tuple-element.573), channel_id=1, source_target_pairs={{0,1},{1,2},{2,3},{3,4},{4,5},{5,6},{6,7},{7,8},{8,9},{9,10},{10,1... | collective-permute-start | bytes 737288 | tf_op jit(solution)/shard_map/while/body/eval_jaxpr/ppermute | solution.py:24
  542.7 11.3 %collective-permute-start = (f32[4,2,12,384]{3,2,1,0:T(8,128)}, f32[4,2,12,384]{3,2,1,0:T(8,128)}, u32[]{:S(2)}, u32[]{:S(2)}) collective-permute-start(f32[4,2,12,384]{3,2,1,0:T(8,128)} %get-tuple-element.570), channel_id=1, source_target_pairs={{0,16},{16,32},{32,48},{48,64},{64,80},{80,96},{96,112},{112,0},{1... | collective-permute-start | bytes 442376 | tf_op jit(solution)/shard_map/while/body/eval_jaxpr/ppermute | solution.py:24
  542.7 12.4 %collective-permute-start.1 = (f32[4,2,12,384]{3,2,1,0:T(8,128)}, f32[4,2,12,384]{3,2,1,0:T(8,128)}, u32[]{:S(2)}, u32[]{:S(2)}) collective-permute-start(f32[4,2,12,384]{3,2,1,0:T(8,128)} %get-tuple-element.571), channel_id=1, source_target_pairs={{16,0},{32,16},{48,32},{64,48},{80,64},{96,80},{112,96},{0,112},{1... | collective-permute-start | bytes 442376 | tf_op jit(solution)/shard_map/while/body/eval_jaxpr/ppermute | solution.py:27
  556.2 11.2 %collective-permute-start.2 = (f32[4,20,2,384]{3,2,1,0:T(2,128)S(1)}, f32[4,20,2,384]{3,2,1,0:T(2,128)S(1)}, u32[]{:S(2)}, u32[]{:S(2)}) collective-permute-start(f32[4,20,2,384]{3,2,1,0:T(2,128)S(1)} %get-tuple-element.572), channel_id=1, source_target_pairs={{1,0},{2,1},{3,2},{4,3},{5,4},{6,5},{7,6},{8,7},{9,8},{10,9},{11,1... | collective-permute-start | bytes 737288 | tf_op jit(solution)/shard_map/while/body/eval_jaxpr/ppermute | solution.py:27
  558.1 10.5 %collective-permute-start.3 = (f32[4,20,2,384]{3,2,1,0:T(2,128)S(1)}, f32[4,20,2,384]{3,2,1,0:T(2,128)S(1)}, u32[]{:S(2)}, u32[]{:S(2)}) collective-permute-start(f32[4,20,2,384]{3,2,1,0:T(2,128)S(1)} %get-tuple-element.573), channel_id=1, source_target_pairs={{0,1},{1,2},{2,3},{3,4},{4,5},{5,6},{6,7},{7,8},{8,9},{9,10},{10,1... | collective-permute-start | bytes 737288 | tf_op jit(solution)/shard_map/while/body/eval_jaxpr/ppermute | solution.py:24
  589.5 11.3 %collective-permute-start = (f32[4,2,12,384]{3,2,1,0:T(8,128)}, f32[4,2,12,384]{3,2,1,0:T(8,128)}, u32[]{:S(2)}, u32[]{:S(2)}) collective-permute-start(f32[4,2,12,384]{3,2,1,0:T(8,128)} %get-tuple-element.570), channel_id=1, source_target_pairs={{0,16},{16,32},{32,48},{48,64},{64,80},{80,96},{96,112},{112,0},{1... | collective-permute-start | bytes 442376 | tf_op jit(solution)/shard_map/while/body/eval_jaxpr/ppermute | solution.py:24
  589.5 12.4 %collective-permute-start.1 = (f32[4,2,12,384]{3,2,1,0:T(8,128)}, f32[4,2,12,384]{3,2,1,0:T(8,128)}, u32[]{:S(2)}, u32[]{:S(2)}) collective-permute-start(f32[4,2,12,384]{3,2,1,0:T(8,128)} %get-tuple-element.571), channel_id=1, source_target_pairs={{16,0},{32,16},{48,32},{64,48},{80,64},{96,80},{112,96},{0,112},{1... | collective-permute-start | bytes 442376 | tf_op jit(solution)/shard_map/while/body/eval_jaxpr/ppermute | solution.py:27
  603.0 11.2 %collective-permute-start.2 = (f32[4,20,2,384]{3,2,1,0:T(2,128)S(1)}, f32[4,20,2,384]{3,2,1,0:T(2,128)S(1)}, u32[]{:S(2)}, u32[]{:S(2)}) collective-permute-start(f32[4,20,2,384]{3,2,1,0:T(2,128)S(1)} %get-tuple-element.572), channel_id=1, source_target_pairs={{1,0},{2,1},{3,2},{4,3},{5,4},{6,5},{7,6},{8,7},{9,8},{10,9},{11,1... | collective-permute-start | bytes 737288 | tf_op jit(solution)/shard_map/while/body/eval_jaxpr/ppermute | solution.py:27
  604.9 10.5 %collective-permute-start.3 = (f32[4,20,2,384]{3,2,1,0:T(2,128)S(1)}, f32[4,20,2,384]{3,2,1,0:T(2,128)S(1)}, u32[]{:S(2)}, u32[]{:S(2)}) collective-permute-start(f32[4,20,2,384]{3,2,1,0:T(2,128)S(1)} %get-tuple-element.573), channel_id=1, source_target_pairs={{0,1},{1,2},{2,3},{3,4},{4,5},{5,6},{6,7},{7,8},{8,9},{9,10},{10,1... | collective-permute-start | bytes 737288 | tf_op jit(solution)/shard_map/while/body/eval_jaxpr/ppermute | solution.py:24
  636.2 11.3 %collective-permute-start = (f32[4,2,12,384]{3,2,1,0:T(8,128)}, f32[4,2,12,384]{3,2,1,0:T(8,128)}, u32[]{:S(2)}, u32[]{:S(2)}) collective-permute-start(f32[4,2,12,384]{3,2,1,0:T(8,128)} %get-tuple-element.570), channel_id=1, source_target_pairs={{0,16},{16,32},{32,48},{48,64},{64,80},{80,96},{96,112},{112,0},{1... | collective-permute-start | bytes 442376 | tf_op jit(solution)/shard_map/while/body/eval_jaxpr/ppermute | solution.py:24
  636.2 12.4 %collective-permute-start.1 = (f32[4,2,12,384]{3,2,1,0:T(8,128)}, f32[4,2,12,384]{3,2,1,0:T(8,128)}, u32[]{:S(2)}, u32[]{:S(2)}) collective-permute-start(f32[4,2,12,384]{3,2,1,0:T(8,128)} %get-tuple-element.571), channel_id=1, source_target_pairs={{16,0},{32,16},{48,32},{64,48},{80,64},{96,80},{112,96},{0,112},{1... | collective-permute-start | bytes 442376 | tf_op jit(solution)/shard_map/while/body/eval_jaxpr/ppermute | solution.py:27
  649.7 11.2 %collective-permute-start.2 = (f32[4,20,2,384]{3,2,1,0:T(2,128)S(1)}, f32[4,20,2,384]{3,2,1,0:T(2,128)S(1)}, u32[]{:S(2)}, u32[]{:S(2)}) collective-permute-start(f32[4,20,2,384]{3,2,1,0:T(2,128)S(1)} %get-tuple-element.572), channel_id=1, source_target_pairs={{1,0},{2,1},{3,2},{4,3},{5,4},{6,5},{7,6},{8,7},{9,8},{10,9},{11,1... | collective-permute-start | bytes 737288 | tf_op jit(solution)/shard_map/while/body/eval_jaxpr/ppermute | solution.py:27
  651.6 10.5 %collective-permute-start.3 = (f32[4,20,2,384]{3,2,1,0:T(2,128)S(1)}, f32[4,20,2,384]{3,2,1,0:T(2,128)S(1)}, u32[]{:S(2)}, u32[]{:S(2)}) collective-permute-start(f32[4,20,2,384]{3,2,1,0:T(2,128)S(1)} %get-tuple-element.573), channel_id=1, source_target_pairs={{0,1},{1,2},{2,3},{3,4},{4,5},{5,6},{6,7},{7,8},{8,9},{9,10},{10,1... | collective-permute-start | bytes 737288 | tf_op jit(solution)/shard_map/while/body/eval_jaxpr/ppermute | solution.py:24
  683.0 11.3 %collective-permute-start = (f32[4,2,12,384]{3,2,1,0:T(8,128)}, f32[4,2,12,384]{3,2,1,0:T(8,128)}, u32[]{:S(2)}, u32[]{:S(2)}) collective-permute-start(f32[4,2,12,384]{3,2,1,0:T(8,128)} %get-tuple-element.570), channel_id=1, source_target_pairs={{0,16},{16,32},{32,48},{48,64},{64,80},{80,96},{96,112},{112,0},{1... | collective-permute-start | bytes 442376 | tf_op jit(solution)/shard_map/while/body/eval_jaxpr/ppermute | solution.py:24
  683.0 12.4 %collective-permute-start.1 = (f32[4,2,12,384]{3,2,1,0:T(8,128)}, f32[4,2,12,384]{3,2,1,0:T(8,128)}, u32[]{:S(2)}, u32[]{:S(2)}) collective-permute-start(f32[4,2,12,384]{3,2,1,0:T(8,128)} %get-tuple-element.571), channel_id=1, source_target_pairs={{16,0},{32,16},{48,32},{64,48},{80,64},{96,80},{112,96},{0,112},{1... | collective-permute-start | bytes 442376 | tf_op jit(solution)/shard_map/while/body/eval_jaxpr/ppermute | solution.py:27
  696.5 11.2 %collective-permute-start.2 = (f32[4,20,2,384]{3,2,1,0:T(2,128)S(1)}, f32[4,20,2,384]{3,2,1,0:T(2,128)S(1)}, u32[]{:S(2)}, u32[]{:S(2)}) collective-permute-start(f32[4,20,2,384]{3,2,1,0:T(2,128)S(1)} %get-tuple-element.572), channel_id=1, source_target_pairs={{1,0},{2,1},{3,2},{4,3},{5,4},{6,5},{7,6},{8,7},{9,8},{10,9},{11,1... | collective-permute-start | bytes 737288 | tf_op jit(solution)/shard_map/while/body/eval_jaxpr/ppermute | solution.py:27
  698.4 10.5 %collective-permute-start.3 = (f32[4,20,2,384]{3,2,1,0:T(2,128)S(1)}, f32[4,20,2,384]{3,2,1,0:T(2,128)S(1)}, u32[]{:S(2)}, u32[]{:S(2)}) collective-permute-start(f32[4,20,2,384]{3,2,1,0:T(2,128)S(1)} %get-tuple-element.573), channel_id=1, source_target_pairs={{0,1},{1,2},{2,3},{3,4},{4,5},{5,6},{6,7},{7,8},{8,9},{9,10},{10,1... | collective-permute-start | bytes 737288 | tf_op jit(solution)/shard_map/while/body/eval_jaxpr/ppermute | solution.py:24
  729.7 11.3 %collective-permute-start = (f32[4,2,12,384]{3,2,1,0:T(8,128)}, f32[4,2,12,384]{3,2,1,0:T(8,128)}, u32[]{:S(2)}, u32[]{:S(2)}) collective-permute-start(f32[4,2,12,384]{3,2,1,0:T(8,128)} %get-tuple-element.570), channel_id=1, source_target_pairs={{0,16},{16,32},{32,48},{48,64},{64,80},{80,96},{96,112},{112,0},{1... | collective-permute-start | bytes 442376 | tf_op jit(solution)/shard_map/while/body/eval_jaxpr/ppermute | solution.py:24
  729.7 12.4 %collective-permute-start.1 = (f32[4,2,12,384]{3,2,1,0:T(8,128)}, f32[4,2,12,384]{3,2,1,0:T(8,128)}, u32[]{:S(2)}, u32[]{:S(2)}) collective-permute-start(f32[4,2,12,384]{3,2,1,0:T(8,128)} %get-tuple-element.571), channel_id=1, source_target_pairs={{16,0},{32,16},{48,32},{64,48},{80,64},{96,80},{112,96},{0,112},{1... | collective-permute-start | bytes 442376 | tf_op jit(solution)/shard_map/while/body/eval_jaxpr/ppermute | solution.py:27
  743.2 11.2 %collective-permute-start.2 = (f32[4,20,2,384]{3,2,1,0:T(2,128)S(1)}, f32[4,20,2,384]{3,2,1,0:T(2,128)S(1)}, u32[]{:S(2)}, u32[]{:S(2)}) collective-permute-start(f32[4,20,2,384]{3,2,1,0:T(2,128)S(1)} %get-tuple-element.572), channel_id=1, source_target_pairs={{1,0},{2,1},{3,2},{4,3},{5,4},{6,5},{7,6},{8,7},{9,8},{10,9},{11,1... | collective-permute-start | bytes 737288 | tf_op jit(solution)/shard_map/while/body/eval_jaxpr/ppermute | solution.py:27
  745.1 10.5 %collective-permute-start.3 = (f32[4,20,2,384]{3,2,1,0:T(2,128)S(1)}, f32[4,20,2,384]{3,2,1,0:T(2,128)S(1)}, u32[]{:S(2)}, u32[]{:S(2)}) collective-permute-start(f32[4,20,2,384]{3,2,1,0:T(2,128)S(1)} %get-tuple-element.573), channel_id=1, source_target_pairs={{0,1},{1,2},{2,3},{3,4},{4,5},{5,6},{6,7},{7,8},{8,9},{9,10},{10,1... | collective-permute-start | bytes 737288 | tf_op jit(solution)/shard_map/while/body/eval_jaxpr/ppermute | solution.py:24
  775.7 27.8 %collective-permute-start.8 = (f32[4,2,12,384]{3,2,1,0:T(8,128)S(1)}, f32[4,2,12,384]{3,2,1,0:T(8,128)S(1)}, u32[]{:S(2)}, u32[]{:S(2)}) collective-permute-start(f32[4,2,12,384]{3,2,1,0:T(8,128)S(1)} %get-tuple-element.414), channel_id=1, source_target_pairs={{0,16},{16,32},{32,48},{48,64},{64,80},{80,96},{96,112},{112,0},{1... | collective-permute-start | bytes 442376 | tf_op jit(solution)/shard_map/ppermute | solution.py:24
  803.9 11.0 %collective-permute-start.10 = (f32[4,20,2,384]{3,2,1,0:T(2,128)S(1)}, f32[4,20,2,384]{3,2,1,0:T(2,128)S(1)}, u32[]{:S(2)}, u32[]{:S(2)}) collective-permute-start(f32[4,20,2,384]{3,2,1,0:T(2,128)S(1)} %get-tuple-element.409), channel_id=1, source_target_pairs={{0,1},{1,2},{2,3},{3,4},{4,5},{5,6},{6,7},{7,8},{8,9},{9,10},{10,1... | collective-permute-start | bytes 737288 | tf_op jit(solution)/shard_map/ppermute | solution.py:24
  811.2 11.9 %collective-permute-start.11 = (f32[4,20,2,384]{3,2,1,0:T(2,128)S(1)}, f32[4,20,2,384]{3,2,1,0:T(2,128)S(1)}, u32[]{:S(2)}, u32[]{:S(2)}) collective-permute-start(f32[4,20,2,384]{3,2,1,0:T(2,128)S(1)} %get-tuple-element.410), channel_id=1, source_target_pairs={{1,0},{2,1},{3,2},{4,3},{5,4},{6,5},{7,6},{8,7},{9,8},{10,9},{11,1... | collective-permute-start | bytes 737288 | tf_op jit(solution)/shard_map/ppermute | solution.py:27
  (156 other events, 545.4 us)
where the time goes:
time: 941 us; the launch traced here: 926 us
  other arithmetic  441 us (47%)
  starting transfers between devices  217 us (23%)
  local copies, waits for them, and re-layouts  201 us (21%)
  waiting for transfers between devices  40.1 us (4%)
  blocking collectives  22.2 us (2%)
    mul x16, other arithmetic, colour_step(): scaled = momentum * inverse  173 us
    mul x48, other arithmetic, residuals(): coupling = weight * blend(viscous, moved(viscous, step_x, step_y, step_z))  130 us
    ppermute x36, starting transfers between devices, extended_2(): lax.ppermute(lax.slice_in_dim(block, block.shape[dim] - width, None, axis...  122 us
    ppermute x36, starting transfers between devices, extended_2(): lax.ppermute(lax.slice_in_dim(block, 0, width, axis=dim), axis, backward)  95.4 us
    while x256, local copies, waits for them, and re-layouts  50.3 us
    ppermute x36, waiting for transfers between devices, extended_2(): lax.ppermute(lax.slice_in_dim(block, block.shape[dim] - width, None, axis...  26.1 us
    all_gather x1, blocking collectives, body(): shard_piece = lax.all_gather(coarse, 'lon', axis=0, tiled=True)  22.2 us
    broadcast_in_dim x16, other arithmetic, colour_step(): return jnp.concatenate([velocity, pressure[None]], axis=0)  21.3 us
  transfers between devices with their start and end apart: 72, of which 36 were waited for; matrix products, arithmetic and copies ran while one was open for 21% of the time, Pallas kernels for 0%

commit v1 on v0

v1 whole, which is shorter than its diff:
```python
import functools
import math

import jax
import jax.numpy as jnp
from jax import lax
from jax.experimental import pallas as pl
from jax.experimental.pallas import tpu as pltpu
from jax.sharding import PartitionSpec as P

SWEEPS = 2
COLOURS = 8
STEPS = SWEEPS * COLOURS
DAMP = 0.6
GAIN = 0.25
NEW = 6
FIRST = 16
MESH = pl.DeviceIdType.MESH
DIRECTIONS = ((1, 0), (-1, 0), (0, 1), (0, -1), (1, 1), (1, -1), (-1, 1), (-1, -1))


def opposite(n):
    return DIRECTIONS.index((-DIRECTIONS[n][0], -DIRECTIONS[n][1]))


def kslot(dx, dy, dz):
    return ((dx + 1) * 3 + (dy + 1)) * 3 + (dz + 1)


def cycle_kernel(cells):
    rate = 4.0 / cells
    screening = 2.0 * math.cosh(rate) - 2.0
    factor = screening / (2.0 * math.sinh(rate) * math.sinh(rate * cells / 2.0))
    return [factor * math.cosh(rate * (cells / 2.0 - d)) for d in range(cells)]


def kernel(
    lon_n,
    lat_n,
    order_ref,
    vis,
    force,
    start_ref,
    vel_out,
    p_out,
    slots,
    coup,
    diag,
    inv,
    winv,
    send_x,
    send_y,
    send_c,
    recv_x,
    recv_y,
    recv_c,
    gathered,
    shared,
    load_sem,
    send_sem,
    recv_sem,
    gsend_sem,
    grecv_sem,
):
    lon = lax.axis_index("lon")
    lat = lax.axis_index("lat")
    planes = vis.shape[0]
    depth = vis.shape[-1]
    blocks = planes // 2 - 2
    tile = (8, depth)
    rows = lax.broadcasted_iota(jnp.int32, tile, 0)
    lanes = lax.broadcasted_iota(jnp.int32, tile, 1)

    def roll_rows(v, up):
        return pltpu.roll(v, up % 8, 0)

    def roll_lanes(v, up):
        return pltpu.roll(v, up % depth, 1)

    def above_z(v):
        return jnp.where(lanes == depth - 1, 0.0, roll_lanes(v, -1))

    def below_z(v):
        return jnp.where(lanes == 0, 0.0, roll_lanes(v, 1))

    def partner(n):
        dx, dy = DIRECTIONS[n]
        return (lax.rem(lon + dx + lon_n, lon_n), lat + dy)

    def present(n):
        dy = DIRECTIONS[n][1]
        if dy > 0:
            return lat < lat_n - 1
        if dy < 0:
            return lat > 0
        return None

    def guarded(cond, fn):
        if cond is None:
            fn()
        else:
            pl.when(cond)(fn)

    load = pltpu.make_async_copy(
        start_ref, slots.at[pl.ds(0, FIRST), pl.ds(1, blocks + 2)], load_sem
    )
    load.start()
    load.wait()

    barrier = pltpu.get_barrier_semaphore()
    for n in range(8):

        def greet(n=n):
            pl.semaphore_signal(barrier, inc=1, device_id=partner(n), device_id_type=MESH)

        guarded(present(n), greet)
    for hop in range(2, lon_n - 1):
        pl.semaphore_signal(
            barrier, inc=1, device_id=(lax.rem(lon + hop, lon_n), lat), device_id_type=MESH
        )
    ends = (lat == 0).astype(jnp.int32) + (lat == lat_n - 1).astype(jnp.int32)
    pl.semaphore_wait(barrier, lon_n + 5 - 3 * ends)

    def inside(yp):
        y = lat * 12 + 2 * (rows - 1) + yp
        return (y >= 0) & (y < 12 * lat_n)

    half = [(1, dy, dz) for dy in (-1, 0, 1) for dz in (-1, 0, 1)]
    half += [(0, 1, dz) for dz in (-1, 0, 1)] + [(0, 0, 1)]

    def couple(x, carry):
        for yp in (0, 1):
            own = vis[x, yp]
            for dx in (0, 1):
                for dy in (-1, 0, 1):
                    offsets = [o for o in half if o[0] == dx and o[1] == dy]
                    if not offsets:
                        continue
                    other_yp = yp if dy == 0 else 1 - yp
                    shift = 0
                    if dy == 1 and yp == 1:
                        shift = -1
                    if dy == -1 and yp == 0:
                        shift = 1
                    other = vis[x + dx, other_yp]
                    if shift:
                        other = roll_rows(other, shift)
                    for o in offsets:
                        dz = o[2]
                        beside = other
                        if dz == 1:
                            beside = above_z(other)
                        elif dz == -1:
                            beside = below_z(other)
                        reach = abs(dx) + abs(dy) + abs(dz)
                        scale = 2.0 * 0.5 ** (reach - 1)
                        value = (scale * own) * beside / jnp.maximum(own + beside, 1.0)
                        coup[kslot(*o), x, yp] = value
                        back = value
                        if dz:
                            back = roll_lanes(back, dz)
                        if shift:
                            back = roll_rows(back, -shift)
                        coup[kslot(-dx, -dy, -dz), x + dx, other_yp] = back
        return carry

    lax.fori_loop(1, planes - 1, couple, 0)

    def diagonal(x, carry):
        for yp in (0, 1):
            total = jnp.zeros(tile, jnp.float32)
            for n in range(27):
                if n != 13:
                    total = total + coup[n, x, yp]
            diag[x, yp] = total
            ok = inside(yp) & (total > 0)
            inv[x, yp] = jnp.where(ok, 1.0 / jnp.where(ok, total, 1.0), 0.0)
        return carry

    lax.fori_loop(2, planes - 1, diagonal, 0)

    def weights(x, carry):
        for yp in (0, 1):
            own = inv[x, yp]
            up = inv[x, 1 - yp]
            if yp == 1:
                up = roll_rows(up, -1)
            total = 3.0 * own + inv[x + 1, yp] + up + above_z(own)
            ok = inside(yp) & (total > 0)
            winv[x, yp] = jnp.where(ok, 1.0 / jnp.where(ok, total, 1.0), 0.0)
        return carry

    lax.fori_loop(2, planes - 2, weights, 0)

    def coupled(x, t, fields):
        at_low = t == 0

        def turn(v):
            return jnp.where(at_low, roll_rows(v, 1), roll_rows(v, -1))

        sums = [[None] * 3 for _ in fields]

        def gather(dy, yp, near):
            for dx in (-1, 0, 1):
                tiles = [f(dx, near) for f in fields]
                for dz in (-1, 0, 1):
                    if near and dx == 0 and dz == 0:
                        continue
                    k = coup[((1 - dx) * 3 + (1 - dy)) * 3 + (1 - dz), x + dx, yp]
                    for n, v in enumerate(tiles):
                        term = k * v
                        old = sums[n][dz + 1]
                        sums[n][dz + 1] = term if old is None else old + term

        gather(jnp.where(at_low, -1, 1), 1 - t, 0)
        for n in range(len(fields)):
            sums[n] = [turn(v) for v in sums[n]]
        gather(jnp.where(at_low, 1, -1), 1 - t, 0)
        gather(0, t, 1)
        return [s[1] + roll_lanes(s[2], -1) + roll_lanes(s[0], 1) for s in sums]

    def pick(table, xp, yp):
        low = jnp.where(yp == 0, table[0], table[1])
        high = jnp.where(yp == 0, table[2], table[3])
        return jnp.where(xp == 0, low, high)

    def sweep(s, table):
        colour = order_ref[lax.rem(s, COLOURS)]
        a = colour & 1
        b = (colour >> 1) & 1
        c = (colour >> 2) & 1
        base = FIRST + NEW * s
        side = s
        rel = {}
        for f in range(4):
            for xr in (0, 1):
                for yr in (0, 1):
                    rel[f, xr, yr] = pick(table[f * 4 : f * 4 + 4], a ^ xr, b ^ yr)
        shift = {
            (xr, yr): pick(table[16:20], a ^ xr, b ^ yr) for xr in (0, 1) for yr in (0, 1)
        }

        def field(f, xr, yr, block):
            index = block + 1
            if f == 0:
                index = index + shift[xr, yr]
            return slots[rel[f, xr, yr], index]

        zmask = (lanes & 1) == c
        z3 = (lanes > 0) | (c == 0)
        ymask = lat * 12 + 2 * (rows - 1) + (1 - b) >= 1
        low = b == 0

        def block_step(block, carry):
            x = 2 * block + a

            def main(f):
                def get(dx, near):
                    at = block if dx == 0 else (block - 1 + a if dx < 0 else block + a)
                    return field(f, abs(dx), 0 if near else 1, at)

                return get

            def xprime(dx, near):
                at = block + a if dx == 0 else (block if dx < 0 else block + 1)
                return field(0, 1 - abs(dx), 0 if near else 1, at)

            def yprime(dx, near):
                at = block if dx == 0 else (block - 1 + a if dx < 0 else block + a)
                return field(1, abs(dx), 1 if near else 0, at)

            p0 = field(3, 0, 0, block)
            p_x = field(3, 1, 0, block - 1 + a)
            p_x1 = field(3, 1, 0, block + a)
            p_y1 = field(3, 0, 1, block)
            k1, k2, k3 = coupled(x, b, [main(0), main(1), main(2)])
            own_inv = inv[x, b]
            p_y = jnp.where(low, roll_rows(p_y1, 1), p_y1)
            g1 = own_inv * (force[0, x, b] + k1 + (p0 - p_x))
            g2 = own_inv * (force[1, x, b] + k2 + (p0 - p_y))
            g3 = own_inv * (force[2, x, b] + k3 + (p0 - below_z(p0)))
            (kx,) = coupled(x + 1, b, [xprime])
            inv_x = inv[x + 1, b]
            gx = inv_x * (force[0, x + 1, b] + kx + (p_x1 - p0))
            (ky,) = coupled(x, 1 - b, [yprime])
            inv_y = inv[x, 1 - b]
            gy = inv_y * (force[1, x, 1 - b] + ky + (p_y1 - jnp.where(low, p0, roll_rows(p0, 1))))
            spread = (gx - g1) + (jnp.where(low, gy, roll_rows(gy, -1)) - g2) + (above_z(g3) - g3)
            dp = jnp.where(zmask, spread * winv[x, b], 0.0)
            dp_y = jnp.where(low, dp, roll_rows(dp, 1))
            keep = 1.0 - DAMP
            u1 = field(0, 0, 0, block)
            u2 = field(1, 0, 0, block)
            u3 = field(2, 0, 0, block)
            ux = field(0, 1, 0, block + a)
            uy = field(1, 0, 1, block)
            push = own_inv * dp
            slots[base + 0, block + 1] = jnp.where(zmask, keep * u1 + DAMP * (g1 + push), u1)
            slots[base + 1, block + 1] = jnp.where(zmask, keep * u2 + DAMP * (g2 + push), u2)
            slots[base + 2, block + 1] = jnp.where(
                z3, keep * u3 + DAMP * (g3 + own_inv * (dp - below_z(dp))), u3
            )
            slots[base + 3, block + 1] = p0 + DAMP * dp
            slots[base + 4, block + 1] = jnp.where(
                zmask & ymask, keep * uy + DAMP * (gy - inv_y * dp_y), uy
            )
            slots[base + 5, block + 1] = jnp.where(zmask, keep * ux + DAMP * (gx - inv_x * dp), ux)
            return carry

        lax.fori_loop(1, blocks + 1, block_step, 0)

        for k in range(NEW):
            send_x[side, 0, k] = slots[base + k, blocks + 1]
            send_x[side, 1, k] = slots[base + k, 2]
            for block in range(1, blocks + 1):
                send_y[side, 0, k, block - 1 : block] = slots[base + k, block + 1, 6:7]
                send_y[side, 1, k, block - 1 : block] = slots[base + k, block + 1, 1:2]
            for n in range(4):
                dx, dy = DIRECTIONS[4 + n]
                row = 6 if dy > 0 else 1
                send_c[side, n, k : k + 1] = slots[
                    base + k, blocks + 1 if dx > 0 else 2, row : row + 1
                ]

        def copy(n):
            if n < 2:
                src, dst = send_x.at[side, n], recv_x.at[side, n]
            elif n < 4:
                src, dst = send_y.at[side, n - 2], recv_y.at[side, n - 2]
            else:
                src, dst = send_c.at[side, n - 4], recv_c.at[side, n - 4]
            return pltpu.make_async_remote_copy(
                src_ref=src,
                dst_ref=dst,
                send_sem=send_sem.at[side, n],
                recv_sem=recv_sem.at[side, n],
                device_id=partner(n),
                device_id_type=MESH,
            )

        for n in (4, 5, 6, 7, 2, 3, 0, 1):
            guarded(present(n), lambda n=n: copy(n).start())
        for n in range(8):
            guarded(present(n), lambda n=n: copy(n).wait_send())
        for n in range(8):
            guarded(present(opposite(n)), lambda n=n: copy(n).wait_recv())

        has_low = lat > 0
        has_high = lat < lat_n - 1
        for k in range(NEW):
            for way, at, low_c, high_c in ((0, 1, 0, 1), (1, blocks + 2, 2, 3)):
                v = recv_x[side, way, k]
                v = jnp.where((rows == 0) & has_low, recv_c[side, low_c, k : k + 1], v)
                v = jnp.where((rows == 7) & has_high, recv_c[side, high_c, k : k + 1], v)
                slots[base + k, at] = v

        @pl.when(has_low)
        def _():
            for k in range(NEW):
                for block in range(1, blocks + 1):
                    slots[base + k, block + 1, 0:1] = recv_y[side, 0, k, block - 1 : block]

        @pl.when(has_high)
        def _():
            for k in range(NEW):
                for block in range(1, blocks + 1):
                    slots[base + k, block + 1, 7:8] = recv_y[side, 1, k, block - 1 : block]

        new = list(table)
        for xp in (0, 1):
            for yp in (0, 1):
                at = xp * 2 + yp
                same = (a == xp) & (b == yp)
                x_next = (a != xp) & (b == yp)
                y_next = (a == xp) & (b != yp)
                new[at] = jnp.where(same, base, jnp.where(x_next, base + 5, table[at]))
                new[16 + at] = jnp.where(same, 0, jnp.where(x_next, -a, table[16 + at]))
                new[4 + at] = jnp.where(same, base + 1, jnp.where(y_next, base + 4, table[4 + at]))
                new[8 + at] = jnp.where(same, base + 2, table[8 + at])
                new[12 + at] = jnp.where(same, base + 3, table[12 + at])
        return tuple(new)

    table = tuple(jnp.int32(n) for n in range(16)) + tuple(jnp.int32(0) for _ in range(4))
    table = lax.fori_loop(0, STEPS, sweep, table)

    def final(f, xp, yp, block):
        index = block + 1
        if f == 0:
            index = index + table[16 + xp * 2 + yp]
        return slots[table[f * 4 + xp * 2 + yp], index]

    def residual_sums(block, sums):
        sums = list(sums)
        for xp in (0, 1):
            for yp in (0, 1):
                x = 2 * block + xp

                def getter(f, xp=xp, yp=yp):
                    def get(dx, near):
                        at = block + (xp + dx) // 2
                        return final(f, (xp + dx) % 2, yp if near else 1 - yp, at)

                    return get

                ks = coupled(x, yp, [getter(0), getter(1), getter(2)])
                p0 = final(3, xp, yp, block)
                p_x = final(3, 1 - xp, yp, block - 1 + xp)
                p_y = final(3, xp, 1 - yp, block)
                if yp == 0:
                    p_y = roll_rows(p_y, 1)
                before = (p_x, p_y, below_z(p0))
                for d in range(3):
                    u = final(d, xp, yp, block)
                    mom = force[d, x, yp] - (diag[x, yp] * u - ks[d]) - (before[d] - p0)
                    sums[d] = sums[d] + mom
                sums[3] = sums[3] + vis[x, yp]
        return tuple(sums)

    odd_row = (rows & 1) == 1
    packed = []
    for part in range(2):
        zero = jnp.zeros(tile, jnp.float32)
        sums = lax.fori_loop(
            part * 4 + 1, part * 4 + 5, residual_sums, (zero, zero, zero, zero)
        )

        def collect(v):
            v = v + roll_rows(v, -1)
            v = v + roll_lanes(v, -1)
            return v + roll_lanes(v, -2)

        valid = odd_row & (rows < 7) & ((lanes & 3) == 0)
        below = jnp.where(valid, collect(sums[3]), 1.0)
        both = zero
        for d in range(3):
            value = jnp.where(valid, collect(sums[d]) / below, 0.0)
            both = both + (roll_lanes(value, d) if d else value)
        packed.append(both)
    own_part = packed[0] + roll_rows(packed[1], 1)
    shared[...] = own_part
    gathered[0] = own_part

    def spread_copy(hop):
        return pltpu.make_async_remote_copy(
            src_ref=shared,
            dst_ref=gathered.at[hop],
            send_sem=gsend_sem.at[hop],
            recv_sem=grecv_sem.at[hop],
            device_id=(lax.rem(lon + hop, lon_n), lat),
            device_id_type=MESH,
        )

    for hop in range(1, lon_n):
        spread_copy(hop).start()
    for hop in range(1, lon_n):
        spread_copy(hop).wait()

    cells = 2 * lon_n
    table_k = cycle_kernel(cells)
    smooth = []
    for part in range(2):
        total = jnp.zeros(tile, jnp.float32)
        for hop in range(lon_n):
            odd_k = table_k[(2 * hop + part) % cells]
            even_k = table_k[(2 * hop + part - 1) % cells]
            total = total + jnp.where(odd_row, odd_k, even_k) * gathered[hop]
        total = GAIN * (total + roll_rows(total, -1))
        per = []
        for d in range(3):
            v = jnp.where(odd_row & ((lanes & 3) == d), total, 0.0)
            if d:
                v = roll_lanes(v, -d)
            v = v + roll_lanes(v, 1)
            v = v + roll_lanes(v, 2)
            per.append(v + roll_rows(v, 1))
        smooth.append(per)

    for part in range(2):

        def finish(block, carry, part=part):
            for xp in (0, 1):
                for yp in (0, 1):
                    x = 2 * block + xp - 2
                    for d in range(3):
                        vel_out[d, x, yp] = final(d, xp, yp, block) + smooth[part][d]
                    own = vis[x + 2, yp]
                    p_out[x, yp] = final(3, xp, yp, block) / jnp.where(own > 0, own, 1.0)
            return carry

        lax.fori_loop(part * 4 + 1, part * 4 + 5, finish, 0)


def extended(block, sides, width):
    for axis, dim, periodic in sides:
        count = lax.axis_size(axis)
        forward = [(i, i + 1) for i in range(count - 1)]
        if periodic:
            forward.append((count - 1, 0))
        backward = [(target, source) for source, target in forward]
        low = lax.ppermute(
            lax.slice_in_dim(block, block.shape[dim] - width, None, axis=dim), axis, forward
        )
        high = lax.ppermute(lax.slice_in_dim(block, 0, width, axis=dim), axis, backward)
        block = jnp.concatenate([low, block, high], axis=dim)
    return block


def body(lon_n, lat_n, velocity, pressure_in, viscosity, body_force, colour_order):
    nx, ny, nz = viscosity.shape
    blocks = nx // 2
    stack = jnp.concatenate(
        [velocity, (pressure_in * viscosity)[None], body_force, viscosity[None]], axis=0
    )
    wide = extended(stack, (("lon", 1, True), ("lat", 2, False)), 2)
    wide = wide.reshape(8, nx + 4, 8, 2, nz).transpose(0, 1, 3, 2, 4)
    start = wide[:4].reshape(4, blocks + 2, 2, 2, 8, nz).transpose(0, 2, 3, 1, 4, 5)
    start = start.reshape(FIRST, blocks + 2, 8, nz)
    f32 = jnp.float32
    whole = pl.BlockSpec(memory_space=pltpu.VMEM)
    n_slots = FIRST + NEW * STEPS
    vel, pres = pl.pallas_call(
        functools.partial(kernel, lon_n, lat_n),
        out_shape=(
            jax.ShapeDtypeStruct((3, nx, 2, 8, nz), f32),
            jax.ShapeDtypeStruct((nx, 2, 8, nz), f32),
        ),
        in_specs=[
            pl.BlockSpec(memory_space=pltpu.SMEM),
            whole,
            whole,
            pl.BlockSpec(memory_space=pl.ANY),
        ],
        out_specs=(whole, whole),
        scratch_shapes=[
            pltpu.VMEM((n_slots, blocks + 3, 8, nz), f32),
            pltpu.VMEM((27, nx + 4, 2, 8, nz), f32),
            pltpu.VMEM((nx + 4, 2, 8, nz), f32),
            pltpu.VMEM((nx + 4, 2, 8, nz), f32),
            pltpu.VMEM((nx + 4, 2, 8, nz), f32),
            pltpu.VMEM((STEPS, 2, NEW, 8, nz), f32),
            pltpu.VMEM((STEPS, 2, NEW, 8, nz), f32),
            pltpu.VMEM((STEPS, 4, 8, nz), f32),
            pltpu.VMEM((STEPS, 2, NEW, 8, nz), f32),
            pltpu.VMEM((STEPS, 2, NEW, 8, nz), f32),
            pltpu.VMEM((STEPS, 4, 8, nz), f32),
            pltpu.VMEM((lon_n, 8, nz), f32),
            pltpu.VMEM((8, nz), f32),
            pltpu.SemaphoreType.DMA,
            pltpu.SemaphoreType.DMA((STEPS, 8)),
            pltpu.SemaphoreType.DMA((STEPS, 8)),
            pltpu.SemaphoreType.DMA((lon_n,)),
            pltpu.SemaphoreType.DMA((lon_n,)),
        ],
        compiler_params=pltpu.CompilerParams(
            collective_id=0, has_side_effects=True, vmem_limit_bytes=60 * 1024 * 1024
        ),
        name="vanka",
    )(colour_order, wide[7], wide[4:7], start)
    vel = vel[:, :, :, 1:7].transpose(0, 1, 3, 2, 4).reshape(3, nx, ny, nz)
    pres = pres[:, :, 1:7].transpose(0, 2, 1, 3).reshape(nx, ny, nz)
    return (vel, pres)


def solution(mesh):
    placed = (
        P(None, "lon", "lat", None),
        P("lon", "lat", None),
        P("lon", "lat", None),
        P(None, "lon", "lat", None),
        P(),
    )
    return jax.shard_map(
        functools.partial(body, mesh.shape["lon"], mesh.shape["lat"]),
        mesh=mesh,
        in_specs=placed,
        out_specs=(P(None, "lon", "lat", None), P("lon", "lat", None)),
        check_vma=False,
    )
```

time: 941 us -> 208 us (0.22); the launches traced: 926 us -> 208 us
  other arithmetic: 441 us -> 4.01 us
  starting transfers between devices: 217 us -> 12.4 us
  local copies, waits for them, and re-layouts: 201 us -> 12.4 us
  Pallas kernels: 0 us -> 161 us
  waiting for transfers between devices: 40.1 us -> 17.7 us
  blocking collectives: 22.2 us -> 0 us
    mul x67 -> x0, other arithmetic: 305 us -> none  [the longest x16 173 us: colour_step(): scaled = momentum * inverse]
    ppermute x72 -> x4, starting transfers between devices: 217 us -> 12.4 us  [the longest x2 7.99 us: extended(): lax.ppermute(lax.slice_in_dim(block, block.shape[dim] - width, None, axis...]
    pallas_call x0 -> x1, Pallas kernels: none -> 161 us  [body(): pl.pallas_call(functools.partial(kernel, lon_n, lat_n), out_shape=(jax.Sh...]
    slice x128 -> x2, local copies, waits for them, and re-layouts: 58.1 us -> 1.38 us  [the longest x1 1.21 us: body(): wide[4:7]]
    while x257 -> x0, local copies, waits for them, and re-layouts: 51.7 us -> none
    another operation x33 -> x0, other arithmetic: 40.9 us -> none  [the longest x17 21.2 us: residuals(): jnp.stack([moved(pressure, -unit_step[0], -unit_step[1], -unit_step[2]) -...]
    sub x2 -> x0, other arithmetic: 23.2 us -> none  [the longest x1 17.9 us: residuals(): applied = applied - coupling * moved(velocity, step_x, step_y, step_z)]
    ppermute x72 -> x4, waiting for transfers between devices: 40.1 us -> 17.7 us  [the longest x2 10.4 us: extended(): lax.ppermute(lax.slice_in_dim(block, block.shape[dim] - width, None, axis...]
  transfers between devices with their start and end apart: 72 -> 4, of which waited for: 36 -> 3; matrix products, arithmetic and copies ran while one was open for 21% -> 0% of each run, Pallas kernels for 0% -> 0%
where the time goes in v1:
time: 208 us
  Pallas kernels  161 us (77%)
  waiting for transfers between devices  17.7 us (9%)
  local copies, waits for them, and re-layouts  12.4 us (6%)
  starting transfers between devices  12.4 us (6%)
  other arithmetic  4.01 us (2%)
    pallas_call x1, Pallas kernels, body(): pl.pallas_call(functools.partial(kernel, lon_n, lat_n), out_shape=(jax.Sh...  161 us
    ppermute x2, waiting for transfers between devices, extended(): lax.ppermute(lax.slice_in_dim(block, block.shape[dim] - width, None, axis...  10.4 us
    ppermute x2, starting transfers between devices, extended(): lax.ppermute(lax.slice_in_dim(block, block.shape[dim] - width, None, axis...  7.99 us
    ppermute x2, waiting for transfers between devices, extended(): lax.ppermute(lax.slice_in_dim(block, 0, width, axis=dim), axis, backward)  7.38 us
    ppermute x2, starting transfers between devices, extended(): lax.ppermute(lax.slice_in_dim(block, 0, width, axis=dim), axis, backward)  4.37 us
  transfers between devices with their start and end apart: 4, of which 3 were waited for; matrix products, arithmetic and copies ran while one was open for 0% of the time, Pallas kernels for 0%

profile of v1, /device:TPU:1, one launch (start us, length us, event | category | flops | bytes accessed | tf_op | source)
XLA Modules:
  0.0 207.9 jit_solution(10530215385464521243)
XLA Ops:
  0.6 0.0 copy-start
  0.6 1.3 copy.20
  2.0 1.1 multiply_bitcast_fusion
  3.1 0.3 copy.18
  3.4 1.8 copy.17
  5.2 0.0 copy-done
  5.2 0.6 copy.19
  5.8 0.3 pad_maximum_fusion.10
  6.1 2.2 %collective-permute-start = (f32[8,2,12,384]{3,0,2,1:T(8,128)S(1)}, f32[8,2,12,384]{3,0,2,1:T(8,128)S(1)}, u32[]{:S(2)}, u32[]{:S(2)}) collective-permute-start(f32[8,2,12,384]{3,0,2,1:T(8,128)S(1)} %get-tuple-element.8), channel_id=1, source_target_pairs={{0,16},{16,32},{32,48},{48,64},{64,80},{80,96},{96,112},{112,0},{1... | collective-permute-start | bytes 884744 | tf_op jit(solution)/shard_map/ppermute | solution.py:500
  8.3 2.4 %collective-permute-start.1 = (f32[8,2,12,384]{3,0,2,1:T(8,128)S(1)}, f32[8,2,12,384]{3,0,2,1:T(8,128)S(1)}, u32[]{:S(2)}, u32[]{:S(2)}) collective-permute-start(f32[8,2,12,384]{3,0,2,1:T(8,128)S(1)} %get-tuple-element.9), channel_id=1, source_target_pairs={{16,0},{32,16},{48,32},{64,48},{80,64},{96,80},{112,96},{0,112},{1... | collective-permute-start | bytes 884744 | tf_op jit(solution)/shard_map/ppermute | solution.py:503
  10.7 6.5 %collective-permute-done = f32[8,2,12,384]{3,0,2,1:T(8,128)S(1)} collective-permute-done((f32[8,2,12,384]{3,0,2,1:T(8,128)S(1)}, f32[8,2,12,384]{3,0,2,1:T(8,128)S(1)}, u32[]{:S(2)}, u32[]{:S(2)}) %collective-permute-start) | collective-permute-done | bytes 294944 | tf_op jit(solution)/shard_map/ppermute | solution.py:500
  17.2 0.0 collective-permute-done.1
  17.2 0.3 pad_maximum_fusion.6
  17.6 5.8 %collective-permute-start.2 = (f32[8,20,2,384]{3,0,2,1:T(8,128)S(1)}, f32[8,20,2,384]{3,0,2,1:T(8,128)S(1)}, u32[]{:S(2)}, u32[]{:S(2)}) collective-permute-start(f32[8,20,2,384]{3,0,2,1:T(8,128)S(1)} %get-tuple-element.6), channel_id=1, source_target_pairs={{0,1},{1,2},{2,3},{3,4},{4,5},{5,6},{6,7},{7,8},{8,9},{9,10},{10,1... | collective-permute-start | bytes 1474568 | tf_op jit(solution)/shard_map/ppermute | solution.py:500
  23.4 1.9 collective-permute-start.3
  25.3 3.8 %collective-permute-done.2 = f32[8,20,2,384]{3,0,2,1:T(8,128)S(1)} collective-permute-done((f32[8,20,2,384]{3,0,2,1:T(8,128)S(1)}, f32[8,20,2,384]{3,0,2,1:T(8,128)S(1)}, u32[]{:S(2)}, u32[]{:S(2)}) %collective-permute-start.2) | collective-permute-done | bytes 491552 | tf_op jit(solution)/shard_map/ppermute | solution.py:500
  29.2 7.4 %collective-permute-done.3 = f32[8,20,2,384]{3,0,2,1:T(8,128)S(1)} collective-permute-done((f32[8,20,2,384]{3,0,2,1:T(8,128)S(1)}, f32[8,20,2,384]{3,0,2,1:T(8,128)S(1)}, u32[]{:S(2)}, u32[]{:S(2)}) %collective-permute-start.3) | collective-permute-done | bytes 491552 | tf_op jit(solution)/shard_map/ppermute | solution.py:503
  36.5 2.3 %pad_maximum_fusion = f32[8,20,16,384]{3,0,2,1:T(8,128)S(1)} fusion(f32[8,20,2,384]{3,0,2,1:T(8,128)S(1)} %collective-permute-done.3, f32[8,2,12,384]{3,0,2,1:T(8,128)S(1)} %collective-permute-done.1, f32[1,16,12,384]{3,0,2,1:T(1,128)S(1)} %copy.20, f32[3,16,12,384]{3,0,2,1:T(4,128)S(1)} %copy.19, f32[1,16,12,384]{3,0,2,1:T(1,128)S(1)} %copy.18, ...), kind=kLoop, calls=%fused_computation | loop fusion | flops 6881280 | bytes 7864320 | tf_op jit(solution)/shard_map/concatenate | solution.py:504
  38.8 1.3 copy.26
  40.1 0.8 slice_bitcast_fusion.1.vis
  40.9 1.2 slice.37.force
  42.1 0.2 slice.38
  42.3 1.5 copy.22
  43.8 160.6 %vanka.1 = (f32[3,16,2,8,384]{4,3,2,1,0:T(8,128)}, f32[16,2,8,384]{3,2,1,0:T(8,128)}) custom-call(s32[8]{0:T(128)} %order_ref.1, f32[20,2,8,384]{3,2,1,0:T(8,128)} %slice_bitcast_fusion.1.vis, f32[3,20,2,8,384]{4,3,2,1,0:T(8,128)} %slice.37.force, f32[16,10,8,384]{3,2,1,0:T(8,128)} %bitcast.23), custom_call_target="tpu_custom_call" | custom-call | tf_op jit(solution)/shard_map/vanka/pallas_call | solution.py:521
  204.4 0.0 copy-start.1
  204.4 1.4 slice_bitcast_fusion
  205.9 1.2 copy.23
  207.1 0.0 copy-done.1
  207.1 0.8 copy.24
  (1 shorter events, 0.0 us)
Async XLA Ops:
  0.6 4.5 %copy-start = (f32[3,16,12,384]{3,1,2,0:T(8,128)S(1)}, f32[3,16,12,384]{3,1,2,0:T(8,128)}, u32[]{:S(2)}) copy-start(f32[3,16,12,384]{3,1,2,0:T(8,128)} %param.8) | copy-start | bytes 2654212
  6.1 11.2 %collective-permute-start = (f32[8,2,12,384]{3,0,2,1:T(8,128)S(1)}, f32[8,2,12,384]{3,0,2,1:T(8,128)S(1)}, u32[]{:S(2)}, u32[]{:S(2)}) collective-permute-start(f32[8,2,12,384]{3,0,2,1:T(8,128)S(1)} %get-tuple-element.8), channel_id=1, source_target_pairs={{0,16},{16,32},{32,48},{48,64},{64,80},{80,96},{96,112},{112,0},{1... | collective-permute-start | bytes 884744 | tf_op jit(solution)/shard_map/ppermute | solution.py:500
  8.3 9.0 %collective-permute-start.1 = (f32[8,2,12,384]{3,0,2,1:T(8,128)S(1)}, f32[8,2,12,384]{3,0,2,1:T(8,128)S(1)}, u32[]{:S(2)}, u32[]{:S(2)}) collective-permute-start(f32[8,2,12,384]{3,0,2,1:T(8,128)S(1)} %get-tuple-element.9), channel_id=1, source_target_pairs={{16,0},{32,16},{48,32},{64,48},{80,64},{96,80},{112,96},{0,112},{1... | collective-permute-start | bytes 884744 | tf_op jit(solution)/shard_map/ppermute | solution.py:503
  17.6 11.6 %collective-permute-start.2 = (f32[8,20,2,384]{3,0,2,1:T(8,128)S(1)}, f32[8,20,2,384]{3,0,2,1:T(8,128)S(1)}, u32[]{:S(2)}, u32[]{:S(2)}) collective-permute-start(f32[8,20,2,384]{3,0,2,1:T(8,128)S(1)} %get-tuple-element.6), channel_id=1, source_target_pairs={{0,1},{1,2},{2,3},{3,4},{4,5},{5,6},{6,7},{7,8},{8,9},{9,10},{10,1... | collective-permute-start | bytes 1474568 | tf_op jit(solution)/shard_map/ppermute | solution.py:500
  23.4 13.1 %collective-permute-start.3 = (f32[8,20,2,384]{3,0,2,1:T(8,128)S(1)}, f32[8,20,2,384]{3,0,2,1:T(8,128)S(1)}, u32[]{:S(2)}, u32[]{:S(2)}) collective-permute-start(f32[8,20,2,384]{3,0,2,1:T(8,128)S(1)} %get-tuple-element.7), channel_id=1, source_target_pairs={{1,0},{2,1},{3,2},{4,3},{5,4},{6,5},{7,6},{8,7},{9,8},{10,9},{11,1... | collective-permute-start | bytes 1474568 | tf_op jit(solution)/shard_map/ppermute | solution.py:503
  204.4 2.6 %copy-start.1 = (f32[16,2,8,384]{3,2,1,0:T(8,128)S(1)}, f32[16,2,8,384]{3,2,1,0:T(8,128)}, u32[]{:S(2)}) copy-start(f32[16,2,8,384]{3,2,1,0:T(8,128)} %get-tuple-element.5) | copy-start | bytes 1179652

commit v2 on v1

--- a/solution.py
+++ b/solution.py
@@ -38,11 +38,14 @@
     lon_n,
     lat_n,
     order_ref,
+    vel_in,
+    p_in,
+    vis_in,
+    force_in,
+    vel_out,
+    p_out,
     vis,
     force,
-    start_ref,
-    vel_out,
-    p_out,
     slots,
     coup,
     diag,
@@ -56,7 +59,14 @@
     recv_c,
     gathered,
     shared,
-    load_sem,
+    first_send_x,
+    first_send_y,
+    first_send_c,
+    first_recv_x,
+    first_recv_y,
+    first_recv_c,
+    first_send_sem,
+    first_recv_sem,
     send_sem,
     recv_sem,
     gsend_sem,
@@ -101,12 +111,6 @@
         else:
             pl.when(cond)(fn)
 
-    load = pltpu.make_async_copy(
-        start_ref, slots.at[pl.ds(0, FIRST), pl.ds(1, blocks + 2)], load_sem
-    )
-    load.start()
-    load.wait()
-
     barrier = pltpu.get_barrier_semaphore()
     for n in range(8):
 
@@ -118,8 +122,117 @@
         pl.semaphore_signal(
             barrier, inc=1, device_id=(lax.rem(lon + hop, lon_n), lat), device_id_type=MESH
         )
+
+    blank = jnp.zeros(tile, jnp.float32)
+
+    def clear(x, carry):
+        for yp in (0, 1):
+            vis[x, yp] = blank
+            for d in range(3):
+                force[d, x, yp] = blank
+        return carry
+
+    lax.fori_loop(0, planes, clear, 0)
+
+    def clear_slots(at, carry):
+        for n in range(FIRST):
+            slots[n, at] = blank
+        return carry
+
+    lax.fori_loop(0, blocks + 3, clear_slots, 0)
+
+    def split(block, carry):
+        for xp in (0, 1):
+            x = 2 * block + xp - 2
+            seen = vis_in[x]
+            scaled = p_in[x] * seen
+            for y in range(12):
+                yp, row = y % 2, y // 2 + 1
+                vis[x + 2, yp, row : row + 1] = seen[y : y + 1]
+                slots[12 + xp * 2 + yp, block + 1, row : row + 1] = scaled[y : y + 1]
+                for d in range(3):
+                    slots[d * 4 + xp * 2 + yp, block + 1, row : row + 1] = vel_in[d, x, y : y + 1]
+                    force[d, x + 2, yp, row : row + 1] = force_in[d, x, y : y + 1]
+        return carry
+
+    lax.fori_loop(1, blocks + 1, split, 0)
+
+    def part(f, x, yp):
+        if f == 7:
+            return vis.at[x, yp]
+        if f >= 4:
+            return force.at[f - 4, x, yp]
+        return slots.at[f * 4 + (x % 2) * 2 + yp, x // 2 + 1]
+
+    first_x = (
+        [(f, 1, yp) for f in (7, 0, 1, 2, 3) for yp in (0, 1)],
+        [(f, planes - 2, yp) for f in (7, 4, 0, 1, 2, 3) for yp in (0, 1)]
+        + [(f, planes - 1, yp) for f in (7, 0) for yp in (0, 1)],
+    )
+    first_y = (
+        [(f, 0) for f in (7, 0, 1, 2, 3)] + [(f, 1) for f in (7, 0, 1, 2, 3, 4, 5, 6)],
+        [(f, 0) for f in (7, 0, 1, 2, 3, 5)] + [(f, 1) for f in (7, 1)],
+    )
+    own_planes = planes - 4
+
+    def first_copy(n):
+        if n < 2:
+            size = len(first_x[n])
+            src = first_send_x.at[n, pl.ds(0, size)]
+            dst = first_recv_x.at[n, pl.ds(0, size)]
+        elif n < 4:
+            size = len(first_y[n - 2])
+            src = first_send_y.at[n - 2, pl.ds(0, size)]
+            dst = first_recv_y.at[n - 2, pl.ds(0, size)]
+        else:
+            src, dst = first_send_c.at[n - 4], first_recv_c.at[n - 4]
+        return pltpu.make_async_remote_copy(
+            src_ref=src,
+            dst_ref=dst,
+            send_sem=first_send_sem.at[n],
+            recv_sem=first_recv_sem.at[n],
+            device_id=partner(n),
+            device_id_type=MESH,
+        )
+
+    for way in (0, 1):
+        for k, (f, x, yp) in enumerate(first_x[way]):
+            source = part(f, x + own_planes if way == 0 else x - own_planes, yp)
+            first_send_x[way, k] = source[...]
+            for n in range(4):
+                dx, dy = DIRECTIONS[4 + n]
+                if (dx > 0) == (way == 0):
+                    row = 6 if dy > 0 else 1
+                    first_send_c[n, k : k + 1] = source[row : row + 1]
     ends = (lat == 0).astype(jnp.int32) + (lat == lat_n - 1).astype(jnp.int32)
     pl.semaphore_wait(barrier, lon_n + 5 - 3 * ends)
+    for n in (4, 5, 6, 7, 0, 1):
+        guarded(present(n), lambda n=n: first_copy(n).start())
+    for way in (0, 1):
+        row = 6 if way == 0 else 1
+        for k, (f, yp) in enumerate(first_y[way]):
+            for x in range(own_planes):
+                first_send_y[way, k, x : x + 1] = part(f, x + 2, yp)[row : row + 1]
+        guarded(present(2 + way), lambda n=2 + way: first_copy(n).start())
+    for n in range(8):
+        guarded(present(opposite(n)), lambda n=n: first_copy(n).wait_recv())
+    has_low = lat > 0
+    has_high = lat < lat_n - 1
+    for way in (0, 1):
+        low_c, high_c = (0, 1) if way == 0 else (2, 3)
+        for k, (f, x, yp) in enumerate(first_x[way]):
+            v = first_recv_x[way, k]
+            v = jnp.where((rows == 0) & has_low, first_recv_c[low_c, k : k + 1], v)
+            v = jnp.where((rows == 7) & has_high, first_recv_c[high_c, k : k + 1], v)
+            part(f, x, yp)[...] = v
+
+    def first_rows(way, row):
+        for k, (f, yp) in enumerate(first_y[way]):
+            for x in range(own_planes):
+                part(f, x + 2, yp)[row : row + 1] = first_recv_y[way, k, x : x + 1]
+
+    pl.when(has_low)(lambda: first_rows(0, 0))
+    pl.when(has_high)(lambda: first_rows(1, 7))
 
     def inside(yp):
         y = lat * 12 + 2 * (rows - 1) + yp
@@ -223,6 +336,22 @@
         low = jnp.where(yp == 0, table[0], table[1])
         high = jnp.where(yp == 0, table[2], table[3])
         return jnp.where(xp == 0, low, high)
+
+    def copy(n, side):
+        if n < 2:
+            src, dst = send_x.at[side, n], recv_x.at[side, n]
+        elif n < 4:
+            src, dst = send_y.at[side, n - 2], recv_y.at[side, n - 2]
+        else:
+            src, dst = send_c.at[side, n - 4], recv_c.at[side, n - 4]
+        return pltpu.make_async_remote_copy(
+            src_ref=src,
+            dst_ref=dst,
+            send_sem=send_sem.at[side, n],
+            recv_sem=recv_sem.at[side, n],
+            device_id=partner(n),
+            device_id_type=MESH,
+        )
 
     def sweep(s, table):
         colour = order_ref[lax.rem(s, COLOURS)]
@@ -307,46 +436,28 @@
             slots[base + 5, block + 1] = jnp.where(zmask, keep * ux + DAMP * (gx - inv_x * dp), ux)
             return carry
 
-        lax.fori_loop(1, blocks + 1, block_step, 0)
-
+        lax.fori_loop(0, 2, lambda n, t: block_step(1 + n * (blocks - 1), t), 0)
         for k in range(NEW):
             send_x[side, 0, k] = slots[base + k, blocks + 1]
             send_x[side, 1, k] = slots[base + k, 2]
-            for block in range(1, blocks + 1):
-                send_y[side, 0, k, block - 1 : block] = slots[base + k, block + 1, 6:7]
-                send_y[side, 1, k, block - 1 : block] = slots[base + k, block + 1, 1:2]
             for n in range(4):
                 dx, dy = DIRECTIONS[4 + n]
                 row = 6 if dy > 0 else 1
                 send_c[side, n, k : k + 1] = slots[
                     base + k, blocks + 1 if dx > 0 else 2, row : row + 1
                 ]
-
-        def copy(n):
-            if n < 2:
-                src, dst = send_x.at[side, n], recv_x.at[side, n]
-            elif n < 4:
-                src, dst = send_y.at[side, n - 2], recv_y.at[side, n - 2]
-            else:
-                src, dst = send_c.at[side, n - 4], recv_c.at[side, n - 4]
-            return pltpu.make_async_remote_copy(
-                src_ref=src,
-                dst_ref=dst,
-                send_sem=send_sem.at[side, n],
-                recv_sem=recv_sem.at[side, n],
-                device_id=partner(n),
-                device_id_type=MESH,
-            )
-
-        for n in (4, 5, 6, 7, 2, 3, 0, 1):
-            guarded(present(n), lambda n=n: copy(n).start())
+        for n in (4, 5, 6, 7, 0, 1):
+            guarded(present(n), lambda n=n: copy(n, side).start())
+        lax.fori_loop(2, blocks, block_step, 0, unroll=2)
+        for k in range(NEW):
+            for block in range(1, blocks + 1):
+                send_y[side, 0, k, block - 1 : block] = slots[base + k, block + 1, 6:7]
+                send_y[side, 1, k, block - 1 : block] = slots[base + k, block + 1, 1:2]
+        for n in (2, 3):
+            guarded(present(n), lambda n=n: copy(n, side).start())
         for n in range(8):
-            guarded(present(n), lambda n=n: copy(n).wait_send())
-        for n in range(8):
-            guarded(present(opposite(n)), lambda n=n: copy(n).wait_recv())
-
-        has_low = lat > 0
-        has_high = lat < lat_n - 1
+            guarded(present(opposite(n)), lambda n=n: copy(n, side).wait_recv())
+
         for k in range(NEW):
             for way, at, low_c, high_c in ((0, 1, 0, 1), (1, blocks + 2, 2, 3)):
                 v = recv_x[side, way, k]
@@ -418,10 +529,10 @@
 
     odd_row = (rows & 1) == 1
     packed = []
-    for part in range(2):
+    for half_no in range(2):
         zero = jnp.zeros(tile, jnp.float32)
         sums = lax.fori_loop(
-            part * 4 + 1, part * 4 + 5, residual_sums, (zero, zero, zero, zero)
+            half_no * 4 + 1, half_no * 4 + 5, residual_sums, (zero, zero, zero, zero)
         )
 
         def collect(v):
@@ -455,14 +566,24 @@
     for hop in range(1, lon_n):
         spread_copy(hop).wait()
 
+    for n in range(8):
+        guarded(present(n), lambda n=n: first_copy(n).wait_send())
+
+    def drain(s, carry):
+        for n in range(8):
+            guarded(present(n), lambda n=n: copy(n, s).wait_send())
+        return carry
+
+    lax.fori_loop(0, STEPS, drain, 0)
+
     cells = 2 * lon_n
     table_k = cycle_kernel(cells)
     smooth = []
-    for part in range(2):
+    for half_no in range(2):
         total = jnp.zeros(tile, jnp.float32)
         for hop in range(lon_n):
-            odd_k = table_k[(2 * hop + part) % cells]
-            even_k = table_k[(2 * hop + part - 1) % cells]
+            odd_k = table_k[(2 * hop + half_no) % cells]
+            even_k = table_k[(2 * hop + half_no - 1) % cells]
             total = total + jnp.where(odd_row, odd_k, even_k) * gathered[hop]
         total = GAIN * (total + roll_rows(total, -1))
         per = []
@@ -475,63 +596,44 @@
             per.append(v + roll_rows(v, 1))
         smooth.append(per)
 
-    for part in range(2):
-
-        def finish(block, carry, part=part):
+    for half_no in range(2):
+
+        def finish(block, carry, half_no=half_no):
             for xp in (0, 1):
                 for yp in (0, 1):
                     x = 2 * block + xp - 2
                     for d in range(3):
-                        vel_out[d, x, yp] = final(d, xp, yp, block) + smooth[part][d]
+                        v = final(d, xp, yp, block) + smooth[half_no][d]
+                        for row in range(6):
+                            y = 2 * row + yp
+                            vel_out[d, x, y : y + 1] = v[row + 1 : row + 2]
                     own = vis[x + 2, yp]
-                    p_out[x, yp] = final(3, xp, yp, block) / jnp.where(own > 0, own, 1.0)
+                    v = final(3, xp, yp, block) / jnp.where(own > 0, own, 1.0)
+                    for row in range(6):
+                        y = 2 * row + yp
+                        p_out[x, y : y + 1] = v[row + 1 : row + 2]
             return carry
 
-        lax.fori_loop(part * 4 + 1, part * 4 + 5, finish, 0)
-
-
-def extended(block, sides, width):
-    for axis, dim, periodic in sides:
-        count = lax.axis_size(axis)
-        forward = [(i, i + 1) for i in range(count - 1)]
-        if periodic:
-            forward.append((count - 1, 0))
-        backward = [(target, source) for source, target in forward]
-        low = lax.ppermute(
-            lax.slice_in_dim(block, block.shape[dim] - width, None, axis=dim), axis, forward
-        )
-        high = lax.ppermute(lax.slice_in_dim(block, 0, width, axis=dim), axis, backward)
-        block = jnp.concatenate([low, block, high], axis=dim)
-    return block
+        lax.fori_loop(half_no * 4 + 1, half_no * 4 + 5, finish, 0)
 
 
 def body(lon_n, lat_n, velocity, pressure_in, viscosity, body_force, colour_order):
     nx, ny, nz = viscosity.shape
     blocks = nx // 2
-    stack = jnp.concatenate(
-        [velocity, (pressure_in * viscosity)[None], body_force, viscosity[None]], axis=0
-    )
-    wide = extended(stack, (("lon", 1, True), ("lat", 2, False)), 2)
-    wide = wide.reshape(8, nx + 4, 8, 2, nz).transpose(0, 1, 3, 2, 4)
-    start = wide[:4].reshape(4, blocks + 2, 2, 2, 8, nz).transpose(0, 2, 3, 1, 4, 5)
-    start = start.reshape(FIRST, blocks + 2, 8, nz)
     f32 = jnp.float32
     whole = pl.BlockSpec(memory_space=pltpu.VMEM)
     n_slots = FIRST + NEW * STEPS
-    vel, pres = pl.pallas_call(
+    return pl.pallas_call(
         functools.partial(kernel, lon_n, lat_n),
         out_shape=(
-            jax.ShapeDtypeStruct((3, nx, 2, 8, nz), f32),
-            jax.ShapeDtypeStruct((nx, 2, 8, nz), f32),
+            jax.ShapeDtypeStruct((3, nx, ny, nz), f32),
+            jax.ShapeDtypeStruct((nx, ny, nz), f32),
         ),
-        in_specs=[
-            pl.BlockSpec(memory_space=pltpu.SMEM),
-            whole,
-            whole,
-            pl.BlockSpec(memory_space=pl.ANY),
-        ],
+        in_specs=[pl.BlockSpec(memory_space=pltpu.SMEM)] + [whole] * 4,
         out_specs=(whole, whole),
         scratch_shapes=[
+            pltpu.VMEM((nx + 4, 2, 8, nz), f32),
+            pltpu.VMEM((3, nx + 4, 2, 8, nz), f32),
             pltpu.VMEM((n_slots, blocks + 3, 8, nz), f32),
             pltpu.VMEM((27, nx + 4, 2, 8, nz), f32),
             pltpu.VMEM((nx + 4, 2, 8, nz), f32),
@@ -545,7 +647,14 @@
             pltpu.VMEM((STEPS, 4, 8, nz), f32),
             pltpu.VMEM((lon_n, 8, nz), f32),
             pltpu.VMEM((8, nz), f32),
-            pltpu.SemaphoreType.DMA,
+            pltpu.VMEM((2, 16, 8, nz), f32),
+            pltpu.VMEM((2, 13, nx, nz), f32),
+            pltpu.VMEM((4, 16, nz), f32),
+            pltpu.VMEM((2, 16, 8, nz), f32),
+            pltpu.VMEM((2, 13, nx, nz), f32),
+            pltpu.VMEM((4, 16, nz), f32),
+            pltpu.SemaphoreType.DMA((8,)),
+            pltpu.SemaphoreType.DMA((8,)),
             pltpu.SemaphoreType.DMA((STEPS, 8)),
             pltpu.SemaphoreType.DMA((STEPS, 8)),
             pltpu.SemaphoreType.DMA((lon_n,)),
@@ -555,10 +664,7 @@
             collective_id=0, has_side_effects=True, vmem_limit_bytes=60 * 1024 * 1024
         ),
         name="vanka",
-    )(colour_order, wide[7], wide[4:7], start)
-    vel = vel[:, :, :, 1:7].transpose(0, 1, 3, 2, 4).reshape(3, nx, ny, nz)
-    pres = pres[:, :, 1:7].transpose(0, 2, 1, 3).reshape(nx, ny, nz)
-    return (vel, pres)
+    )(colour_order, velocity, pressure_in, viscosity, body_force)
 
 
 def solution(mesh):

time: 208 us -> 162 us (0.78); the launches traced: 208 us -> 159 us
  waiting for transfers between devices: 17.7 us -> 0 us
  starting transfers between devices: 12.4 us -> 0 us
  Pallas kernels: 161 us -> 149 us
  other arithmetic: 4.01 us -> 0 us
  local copies, waits for them, and re-layouts: 12.4 us -> 9.62 us
    ppermute x4 -> x0, waiting for transfers between devices: 17.7 us -> none  [the longest x2 10.4 us: extended(): lax.ppermute(lax.slice_in_dim(block, block.shape[dim] - width, None, axis...]
    ppermute x4 -> x0, starting transfers between devices: 12.4 us -> none  [the longest x2 7.99 us: extended(): lax.ppermute(lax.slice_in_dim(block, block.shape[dim] - width, None, axis...]
    pallas_call x1, Pallas kernels: 161 us -> 149 us  [body(): pl.pallas_call(functools.partial(kernel, lon_n, lat_n), out_shape=(jax.Sh...]
    unnamed x6 -> x10, local copies, waits for them, and re-layouts: 2.4 us -> 6.32 us
    transpose x4 -> x0, local copies, waits for them, and re-layouts: 3.45 us -> none  [the longest x2 2.61 us: body(): vel = vel[:, :, :, 1:7].transpose(0, 1, 3, 2, 4).reshape(3, nx, ny, nz)]
    pallas_call x0 -> x2, local copies, waits for them, and re-layouts: none -> 3.31 us  [body(): pl.pallas_call(functools.partial(kernel, lon_n, lat_n), out_shape=(jax.Sh...]
    reshape x2 -> x0, local copies, waits for them, and re-layouts: 2.73 us -> none  [the longest x1 1.46 us: body(): wide[:4].reshape(4, blocks + 2, 2, 2, 8, nz).transpose(0, 2, 3, 1, 4, 5)]
    concatenate x1 -> x0, other arithmetic: 2.31 us -> none  [extended(): block = jnp.concatenate([low, block, high], axis=dim)]
  transfers between devices with their start and end apart: 4 -> 0, of which waited for: 3 -> 0; matrix products, arithmetic and copies ran while one was open for 0% -> 0% of each run, Pallas kernels for 0% -> 0%
where the time goes in v2:
time: 162 us; the launch traced here: 159 us
  Pallas kernels  149 us (92%)
  local copies, waits for them, and re-layouts  9.62 us (6%)
    pallas_call x1, Pallas kernels, body(): pl.pallas_call(functools.partial(kernel, lon_n, lat_n), out_shape=(jax.Sh...  149 us
    unnamed x10, local copies, waits for them, and re-layouts  6.32 us
    pallas_call x2, local copies, waits for them, and re-layouts, body(): pl.pallas_call(functools.partial(kernel, lon_n, lat_n), out_shape=(jax.Sh...  3.31 us

profile of v2, /device:TPU:1, one launch (start us, length us, event | category | flops | bytes accessed | tf_op | source)
XLA Modules:
  0.0 159.4 jit_solution(889515849089593694)
XLA Ops:
  0.6 0.0 copy-start
  0.6 1.9 %copy.8.p_in = f32[16,12,384]{2,1,0:T(8,128)} copy(f32[16,12,384]{2,0,1:T(8,128)} %param.6) | data formatting | bytes 589824 | tf_op args[1]
  2.5 1.8 %copy.9.vis_in = f32[16,12,384]{2,1,0:T(8,128)} copy(f32[16,12,384]{2,0,1:T(8,128)} %param.7) | data formatting | bytes 589824 | tf_op args[2]
  4.3 0.0 copy-done
  4.3 0.0 copy-start.1
  4.3 1.3 copy.7.vel_in
  5.6 0.0 copy-done.1
  5.6 1.3 copy.10.force_in
  7.0 149.2 %vanka.1 = (f32[3,16,12,384]{3,2,1,0:T(8,128)}, f32[16,12,384]{2,1,0:T(8,128)}) custom-call(s32[8]{0:T(128)} %order_ref.1, f32[3,16,12,384]{3,2,1,0:T(8,128)} %copy.7.vel_in, f32[16,12,384]{2,1,0:T(8,128)} %copy.8.p_in, f32[16,12,384]{2,1,0:T(8,128)} %copy.9.vis_in, f32[3,16,12,384]{3,2,1,0:T(8,128)} %copy.10.force_in), custom_call_target="tpu_custom_call" | custom-call | tf_op jit(solution)/shard_map/vanka/pallas_call | solution.py:626
  156.1 0.0 copy-start.2
  156.1 2.5 %copy.11 = f32[3,16,12,384]{3,1,2,0:T(8,128)} copy(f32[3,16,12,384]{3,2,1,0:T(8,128)} %get-tuple-element.2) | data formatting | bytes 1769472 | tf_op jit(solution)/shard_map/vanka/pallas_call | solution.py:626
  158.6 0.0 copy-done.2
  158.6 0.8 copy.12
Async XLA Ops:
  0.6 3.7 %copy-start = (f32[3,16,12,384]{3,1,2,0:T(8,128)S(1)}, f32[3,16,12,384]{3,1,2,0:T(8,128)}, u32[]{:S(2)}) copy-start(f32[3,16,12,384]{3,1,2,0:T(8,128)} %param.5) | copy-start | bytes 2654212
  4.3 1.3 copy-start.1
  156.1 2.5 %copy-start.2 = (f32[16,12,384]{2,1,0:T(8,128)S(1)}, f32[16,12,384]{2,1,0:T(8,128)}, u32[]{:S(2)}) copy-start(f32[16,12,384]{2,1,0:T(8,128)} %get-tuple-element.3) | copy-start | bytes 884740

commit v3 on v2

--- a/solution.py
+++ b/solution.py
@@ -13,6 +13,7 @@
 STEPS = SWEEPS * COLOURS
 DAMP = 0.6
 GAIN = 0.25
+SENT = 4
 NEW = 6
 FIRST = 16
 MESH = pl.DeviceIdType.MESH
@@ -38,12 +39,16 @@
     lon_n,
     lat_n,
     order_ref,
+    vel_hbm,
+    p_hbm,
+    vis_hbm,
+    force_hbm,
+    vel_out,
+    p_out,
     vel_in,
     p_in,
     vis_in,
     force_in,
-    vel_out,
-    p_out,
     vis,
     force,
     slots,
@@ -67,6 +72,8 @@
     first_recv_c,
     first_send_sem,
     first_recv_sem,
+    pack,
+    load_sem,
     send_sem,
     recv_sem,
     gsend_sem,
@@ -111,6 +118,11 @@
         else:
             pl.when(cond)(fn)
 
+    pairs = ((vis_hbm, vis_in), (p_hbm, p_in), (vel_hbm, vel_in), (force_hbm, force_in))
+    loads = [pltpu.make_async_copy(src, dst, load_sem.at[n]) for n, (src, dst) in enumerate(pairs)]
+    for copy_in in loads:
+        copy_in.start()
+
     barrier = pltpu.get_barrier_semaphore()
     for n in range(8):
 
@@ -155,6 +167,8 @@
                     force[d, x + 2, yp, row : row + 1] = force_in[d, x, y : y + 1]
         return carry
 
+    for copy_in in loads:
+        copy_in.wait()
     lax.fori_loop(1, blocks + 1, split, 0)
 
     def part(f, x, yp):
@@ -424,58 +438,88 @@
             ux = field(0, 1, 0, block + a)
             uy = field(1, 0, 1, block)
             push = own_inv * dp
-            slots[base + 0, block + 1] = jnp.where(zmask, keep * u1 + DAMP * (g1 + push), u1)
-            slots[base + 1, block + 1] = jnp.where(zmask, keep * u2 + DAMP * (g2 + push), u2)
+            new_1 = jnp.where(zmask, keep * u1 + DAMP * (g1 + push), u1)
+            new_2 = jnp.where(zmask, keep * u2 + DAMP * (g2 + push), u2)
+            new_y = jnp.where(zmask & ymask, keep * uy + DAMP * (gy - inv_y * dp_y), uy)
+            new_x = jnp.where(zmask, keep * ux + DAMP * (gx - inv_x * dp), ux)
+            slots[base + 0, block + 1] = new_1
+            slots[base + 1, block + 1] = new_2
+            pack[0, block] = jnp.where(zmask, new_1, roll_lanes(new_x, 1))
+            pack[1, block] = jnp.where(zmask, new_2, roll_lanes(new_y, 1))
             slots[base + 2, block + 1] = jnp.where(
                 z3, keep * u3 + DAMP * (g3 + own_inv * (dp - below_z(dp))), u3
             )
             slots[base + 3, block + 1] = p0 + DAMP * dp
-            slots[base + 4, block + 1] = jnp.where(
-                zmask & ymask, keep * uy + DAMP * (gy - inv_y * dp_y), uy
-            )
-            slots[base + 5, block + 1] = jnp.where(zmask, keep * ux + DAMP * (gx - inv_x * dp), ux)
+            slots[base + 4, block + 1] = new_y
+            slots[base + 5, block + 1] = new_x
             return carry
 
         lax.fori_loop(0, 2, lambda n, t: block_step(1 + n * (blocks - 1), t), 0)
-        for k in range(NEW):
-            send_x[side, 0, k] = slots[base + k, blocks + 1]
-            send_x[side, 1, k] = slots[base + k, 2]
+
+        def packed_tile(k, block):
+            return pack.at[k, block] if k < 2 else slots.at[base + k, block + 1]
+
+        for k in range(SENT):
+            send_x[side, 0, k] = packed_tile(k, blocks)[...]
+            send_x[side, 1, k] = packed_tile(k, 1)[...]
             for n in range(4):
                 dx, dy = DIRECTIONS[4 + n]
                 row = 6 if dy > 0 else 1
-                send_c[side, n, k : k + 1] = slots[
-                    base + k, blocks + 1 if dx > 0 else 2, row : row + 1
-                ]
+                source = packed_tile(k, blocks if dx > 0 else 1)
+                send_c[side, n, k : k + 1] = source[row : row + 1]
         for n in (4, 5, 6, 7, 0, 1):
             guarded(present(n), lambda n=n: copy(n, side).start())
         lax.fori_loop(2, blocks, block_step, 0, unroll=2)
-        for k in range(NEW):
+        for k in range(SENT):
             for block in range(1, blocks + 1):
-                send_y[side, 0, k, block - 1 : block] = slots[base + k, block + 1, 6:7]
-                send_y[side, 1, k, block - 1 : block] = slots[base + k, block + 1, 1:2]
+                source = packed_tile(k, block)
+                send_y[side, 0, k, block - 1 : block] = source[6:7]
+                send_y[side, 1, k, block - 1 : block] = source[1:2]
         for n in (2, 3):
             guarded(present(n), lambda n=n: copy(n, side).start())
         for n in range(8):
             guarded(present(opposite(n)), lambda n=n: copy(n, side).wait_recv())
 
-        for k in range(NEW):
-            for way, at, low_c, high_c in ((0, 1, 0, 1), (1, blocks + 2, 2, 3)):
+        for way, at, low_c, high_c in ((0, 1, 0, 1), (1, blocks + 2, 2, 3)):
+            tiles = []
+            for k in range(SENT):
                 v = recv_x[side, way, k]
                 v = jnp.where((rows == 0) & has_low, recv_c[side, low_c, k : k + 1], v)
                 v = jnp.where((rows == 7) & has_high, recv_c[side, high_c, k : k + 1], v)
-                slots[base + k, at] = v
-
-        @pl.when(has_low)
-        def _():
-            for k in range(NEW):
+                tiles.append(v)
+            x_index = jnp.minimum(at + a + shift[1, 0], blocks + 2)
+            slots[base + 0, at] = jnp.where(zmask, tiles[0], field(0, 0, 0, at - 1))
+            slots[base + 1, at] = jnp.where(zmask, tiles[1], field(1, 0, 0, at - 1))
+            slots[base + 2, at] = tiles[2]
+            slots[base + 3, at] = tiles[3]
+            slots[base + 4, at] = jnp.where(
+                zmask, roll_lanes(tiles[1], -1), field(1, 0, 1, at - 1)
+            )
+            slots[base + 5, at] = jnp.where(
+                zmask, roll_lanes(tiles[0], -1), slots[rel[0, 1, 0], x_index]
+            )
+
+        zrow = zmask[0:1]
+
+        def margin_rows(way, row):
+            got = [recv_y[side, way, k] for k in range(SENT)]
+            turned = [roll_lanes(got[0], -1), roll_lanes(got[1], -1)]
+            for k, v, mixed in (
+                (0, got[0], True),
+                (1, got[1], True),
+                (2, got[2], False),
+                (3, got[3], False),
+                (4, turned[1], True),
+                (5, turned[0], True),
+            ):
                 for block in range(1, blocks + 1):
-                    slots[base + k, block + 1, 0:1] = recv_y[side, 0, k, block - 1 : block]
-
-        @pl.when(has_high)
-        def _():
-            for k in range(NEW):
-                for block in range(1, blocks + 1):
-                    slots[base + k, block + 1, 7:8] = recv_y[side, 1, k, block - 1 : block]
+                    new_row = v[block - 1 : block]
+                    if mixed:
+                        new_row = jnp.where(zrow, new_row, slots[base + k, block + 1, row : row + 1])
+                    slots[base + k, block + 1, row : row + 1] = new_row
+
+        pl.when(has_low)(lambda: margin_rows(0, 0))
+        pl.when(has_high)(lambda: margin_rows(1, 7))
 
         new = list(table)
         for xp in (0, 1):
@@ -629,9 +673,14 @@
             jax.ShapeDtypeStruct((3, nx, ny, nz), f32),
             jax.ShapeDtypeStruct((nx, ny, nz), f32),
         ),
-        in_specs=[pl.BlockSpec(memory_space=pltpu.SMEM)] + [whole] * 4,
+        in_specs=[pl.BlockSpec(memory_space=pltpu.SMEM)]
+        + [pl.BlockSpec(memory_space=pl.ANY)] * 4,
         out_specs=(whole, whole),
         scratch_shapes=[
+            pltpu.VMEM((3, nx, ny, nz), f32),
+            pltpu.VMEM((nx, ny, nz), f32),
+            pltpu.VMEM((nx, ny, nz), f32),
+            pltpu.VMEM((3, nx, ny, nz), f32),
             pltpu.VMEM((nx + 4, 2, 8, nz), f32),
             pltpu.VMEM((3, nx + 4, 2, 8, nz), f32),
             pltpu.VMEM((n_slots, blocks + 3, 8, nz), f32),
@@ -639,11 +688,11 @@
             pltpu.VMEM((nx + 4, 2, 8, nz), f32),
             pltpu.VMEM((nx + 4, 2, 8, nz), f32),
             pltpu.VMEM((nx + 4, 2, 8, nz), f32),
-            pltpu.VMEM((STEPS, 2, NEW, 8, nz), f32),
-            pltpu.VMEM((STEPS, 2, NEW, 8, nz), f32),
+            pltpu.VMEM((STEPS, 2, SENT, 8, nz), f32),
+            pltpu.VMEM((STEPS, 2, SENT, 8, nz), f32),
             pltpu.VMEM((STEPS, 4, 8, nz), f32),
-            pltpu.VMEM((STEPS, 2, NEW, 8, nz), f32),
-            pltpu.VMEM((STEPS, 2, NEW, 8, nz), f32),
+            pltpu.VMEM((STEPS, 2, SENT, 8, nz), f32),
+            pltpu.VMEM((STEPS, 2, SENT, 8, nz), f32),
             pltpu.VMEM((STEPS, 4, 8, nz), f32),
             pltpu.VMEM((lon_n, 8, nz), f32),
             pltpu.VMEM((8, nz), f32),
@@ -655,6 +704,8 @@
             pltpu.VMEM((4, 16, nz), f32),
             pltpu.SemaphoreType.DMA((8,)),
             pltpu.SemaphoreType.DMA((8,)),
+            pltpu.VMEM((2, blocks + 1, 8, nz), f32),
+            pltpu.SemaphoreType.DMA((4,)),
             pltpu.SemaphoreType.DMA((STEPS, 8)),
             pltpu.SemaphoreType.DMA((STEPS, 8)),
             pltpu.SemaphoreType.DMA((lon_n,)),

time: 162 us -> 154 us (0.951)
  Pallas kernels: 149 us -> 142 us
    pallas_call x1, Pallas kernels: 149 us -> 142 us  [body(): pl.pallas_call(functools.partial(kernel, lon_n, lat_n), out_shape=(jax.Sh...]
where the time goes in v3:
time: 154 us; the launch traced here: 152 us
  Pallas kernels  142 us (92%)
  local copies, waits for them, and re-layouts  9.62 us (6%)
    pallas_call x1, Pallas kernels, body(): pl.pallas_call(functools.partial(kernel, lon_n, lat_n), out_shape=(jax.Sh...  142 us
    unnamed x10, local copies, waits for them, and re-layouts  6.32 us
    pallas_call x2, local copies, waits for them, and re-layouts, body(): pl.pallas_call(functools.partial(kernel, lon_n, lat_n), out_shape=(jax.Sh...  3.31 us

profile of v3, /device:TPU:1, one launch (start us, length us, event | category | flops | bytes accessed | tf_op | source)
XLA Modules:
  0.0 152.0 jit_solution(3812688575232139365)
XLA Ops:
  0.6 0.0 copy-start
  0.6 1.9 %copy.8.p_hbm = f32[16,12,384]{2,1,0:T(8,128)} copy(f32[16,12,384]{2,0,1:T(8,128)} %param.6) | data formatting | bytes 589824 | tf_op args[1]
  2.5 1.8 %copy.9.vis_hbm = f32[16,12,384]{2,1,0:T(8,128)} copy(f32[16,12,384]{2,0,1:T(8,128)} %param.7) | data formatting | bytes 589824 | tf_op args[2]
  4.3 0.0 copy-done
  4.3 0.0 copy-start.1
  4.3 1.3 copy.7.vel_hbm
  5.6 0.0 copy-done.1
  5.6 1.3 copy.10.force_hbm
  7.0 141.7 %vanka.1 = (f32[3,16,12,384]{3,2,1,0:T(8,128)}, f32[16,12,384]{2,1,0:T(8,128)}) custom-call(s32[8]{0:T(128)} %order_ref.1, f32[3,16,12,384]{3,2,1,0:T(8,128)} %copy.7.vel_hbm, f32[16,12,384]{2,1,0:T(8,128)} %copy.8.p_hbm, f32[16,12,384]{2,1,0:T(8,128)} %copy.9.vis_hbm, f32[3,16,12,384]{3,2,1,0:T(8,128)} %copy.10.force_hbm), custom_call_target="tpu_custom_call" | custom-call | tf_op jit(solution)/shard_map/vanka/pallas_call | solution.py:670
  148.7 0.0 copy-start.2
  148.7 2.5 %copy.11 = f32[3,16,12,384]{3,1,2,0:T(8,128)} copy(f32[3,16,12,384]{3,2,1,0:T(8,128)} %get-tuple-element.2) | data formatting | bytes 1769472 | tf_op jit(solution)/shard_map/vanka/pallas_call | solution.py:670
  151.2 0.0 copy-done.2
  151.2 0.8 copy.12
Async XLA Ops:
  0.6 3.7 %copy-start = (f32[3,16,12,384]{3,1,2,0:T(8,128)S(1)}, f32[3,16,12,384]{3,1,2,0:T(8,128)}, u32[]{:S(2)}) copy-start(f32[3,16,12,384]{3,1,2,0:T(8,128)} %param.5) | copy-start | bytes 2654212
  4.3 1.3 copy-start.1
  148.7 2.5 %copy-start.2 = (f32[16,12,384]{2,1,0:T(8,128)S(1)}, f32[16,12,384]{2,1,0:T(8,128)}, u32[]{:S(2)}) copy-start(f32[16,12,384]{2,1,0:T(8,128)} %get-tuple-element.3) | copy-start | bytes 884740

commit v4 on v3

--- a/solution.py
+++ b/solution.py
@@ -179,74 +179,95 @@
         return slots.at[f * 4 + (x % 2) * 2 + yp, x // 2 + 1]
 
     first_x = (
-        [(f, 1, yp) for f in (7, 0, 1, 2, 3) for yp in (0, 1)],
-        [(f, planes - 2, yp) for f in (7, 4, 0, 1, 2, 3) for yp in (0, 1)]
-        + [(f, planes - 1, yp) for f in (7, 0) for yp in (0, 1)],
+        (
+            [(7, 1, yp) for yp in (0, 1)],
+            [(7, x, yp) for x in (planes - 2, planes - 1) for yp in (0, 1)],
+        ),
+        (
+            [(f, 1, yp) for f in (0, 1, 2, 3) for yp in (0, 1)],
+            [(f, planes - 2, yp) for f in (4, 0, 1, 2, 3) for yp in (0, 1)]
+            + [(0, planes - 1, yp) for yp in (0, 1)],
+        ),
     )
     first_y = (
-        [(f, 0) for f in (7, 0, 1, 2, 3)] + [(f, 1) for f in (7, 0, 1, 2, 3, 4, 5, 6)],
-        [(f, 0) for f in (7, 0, 1, 2, 3, 5)] + [(f, 1) for f in (7, 1)],
+        ([(7, 0), (7, 1)], [(7, 0), (7, 1)]),
+        (
+            [(f, 0) for f in (0, 1, 2, 3)] + [(f, 1) for f in (0, 1, 2, 3, 4, 5, 6)],
+            [(f, 0) for f in (0, 1, 2, 3, 5)] + [(1, 1)],
+        ),
     )
     own_planes = planes - 4
 
-    def first_copy(n):
+    def first_copy(part_no, n):
         if n < 2:
-            size = len(first_x[n])
-            src = first_send_x.at[n, pl.ds(0, size)]
-            dst = first_recv_x.at[n, pl.ds(0, size)]
+            at = (part_no, n, pl.ds(0, len(first_x[part_no][n])))
+            src, dst = first_send_x.at[at], first_recv_x.at[at]
         elif n < 4:
-            size = len(first_y[n - 2])
-            src = first_send_y.at[n - 2, pl.ds(0, size)]
-            dst = first_recv_y.at[n - 2, pl.ds(0, size)]
+            at = (part_no, n - 2, pl.ds(0, len(first_y[part_no][n - 2])))
+            src, dst = first_send_y.at[at], first_recv_y.at[at]
         else:
-            src, dst = first_send_c.at[n - 4], first_recv_c.at[n - 4]
+            src, dst = first_send_c.at[part_no, n - 4], first_recv_c.at[part_no, n - 4]
         return pltpu.make_async_remote_copy(
             src_ref=src,
             dst_ref=dst,
-            send_sem=first_send_sem.at[n],
-            recv_sem=first_recv_sem.at[n],
+            send_sem=first_send_sem.at[part_no, n],
+            recv_sem=first_recv_sem.at[part_no, n],
             device_id=partner(n),
             device_id_type=MESH,
         )
 
-    for way in (0, 1):
-        for k, (f, x, yp) in enumerate(first_x[way]):
-            source = part(f, x + own_planes if way == 0 else x - own_planes, yp)
-            first_send_x[way, k] = source[...]
-            for n in range(4):
-                dx, dy = DIRECTIONS[4 + n]
-                if (dx > 0) == (way == 0):
-                    row = 6 if dy > 0 else 1
-                    first_send_c[n, k : k + 1] = source[row : row + 1]
+    def first_stage(part_no):
+        for way in (0, 1):
+            for k, (f, x, yp) in enumerate(first_x[part_no][way]):
+                source = part(f, x + own_planes if way == 0 else x - own_planes, yp)
+                first_send_x[part_no, way, k] = source[...]
+                for n in range(4):
+                    dx, dy = DIRECTIONS[4 + n]
+                    if (dx > 0) == (way == 0):
+                        row = 6 if dy > 0 else 1
+                        first_send_c[part_no, n, k : k + 1] = source[row : row + 1]
+            row = 6 if way == 0 else 1
+            for k, (f, yp) in enumerate(first_y[part_no][way]):
+                for x in range(own_planes):
+                    first_send_y[part_no, way, k, x : x + 1] = part(f, x + 2, yp)[
+                        row : row + 1
+                    ]
+
+    def first_start(part_no):
+        for n in (4, 5, 6, 7, 2, 3, 0, 1):
+            guarded(present(n), lambda n=n: first_copy(part_no, n).start())
+
+    has_low = lat > 0
+    has_high = lat < lat_n - 1
+
+    def first_finish(part_no):
+        for n in range(8):
+            guarded(present(opposite(n)), lambda n=n: first_copy(part_no, n).wait_recv())
+        for way in (0, 1):
+            low_c, high_c = (0, 1) if way == 0 else (2, 3)
+            for k, (f, x, yp) in enumerate(first_x[part_no][way]):
+                v = first_recv_x[part_no, way, k]
+                v = jnp.where((rows == 0) & has_low, first_recv_c[part_no, low_c, k : k + 1], v)
+                v = jnp.where((rows == 7) & has_high, first_recv_c[part_no, high_c, k : k + 1], v)
+                part(f, x, yp)[...] = v
+
+        def first_rows(way, row):
+            for k, (f, yp) in enumerate(first_y[part_no][way]):
+                for x in range(own_planes):
+                    part(f, x + 2, yp)[row : row + 1] = first_recv_y[
+                        part_no, way, k, x : x + 1
+                    ]
+
+        pl.when(has_low)(lambda: first_rows(0, 0))
+        pl.when(has_high)(lambda: first_rows(1, 7))
+
+    first_stage(0)
     ends = (lat == 0).astype(jnp.int32) + (lat == lat_n - 1).astype(jnp.int32)
     pl.semaphore_wait(barrier, lon_n + 5 - 3 * ends)
-    for n in (4, 5, 6, 7, 0, 1):
-        guarded(present(n), lambda n=n: first_copy(n).start())
-    for way in (0, 1):
-        row = 6 if way == 0 else 1
-        for k, (f, yp) in enumerate(first_y[way]):
-            for x in range(own_planes):
-                first_send_y[way, k, x : x + 1] = part(f, x + 2, yp)[row : row + 1]
-        guarded(present(2 + way), lambda n=2 + way: first_copy(n).start())
-    for n in range(8):
-        guarded(present(opposite(n)), lambda n=n: first_copy(n).wait_recv())
-    has_low = lat > 0
-    has_high = lat < lat_n - 1
-    for way in (0, 1):
-        low_c, high_c = (0, 1) if way == 0 else (2, 3)
-        for k, (f, x, yp) in enumerate(first_x[way]):
-            v = first_recv_x[way, k]
-            v = jnp.where((rows == 0) & has_low, first_recv_c[low_c, k : k + 1], v)
-            v = jnp.where((rows == 7) & has_high, first_recv_c[high_c, k : k + 1], v)
-            part(f, x, yp)[...] = v
-
-    def first_rows(way, row):
-        for k, (f, yp) in enumerate(first_y[way]):
-            for x in range(own_planes):
-                part(f, x + 2, yp)[row : row + 1] = first_recv_y[way, k, x : x + 1]
-
-    pl.when(has_low)(lambda: first_rows(0, 0))
-    pl.when(has_high)(lambda: first_rows(1, 7))
+    first_start(0)
+    first_stage(1)
+    first_start(1)
+    first_finish(0)
 
     def inside(yp):
         y = lat * 12 + 2 * (rows - 1) + yp
@@ -318,6 +339,7 @@
         return carry
 
     lax.fori_loop(2, planes - 2, weights, 0)
+    first_finish(1)
 
     def coupled(x, t, fields):
         at_low = t == 0
@@ -610,8 +632,9 @@
     for hop in range(1, lon_n):
         spread_copy(hop).wait()
 
-    for n in range(8):
-        guarded(present(n), lambda n=n: first_copy(n).wait_send())
+    for part_no in (0, 1):
+        for n in range(8):
+            guarded(present(n), lambda p=part_no, n=n: first_copy(p, n).wait_send())
 
     def drain(s, carry):
         for n in range(8):
@@ -696,14 +719,14 @@
             pltpu.VMEM((STEPS, 4, 8, nz), f32),
             pltpu.VMEM((lon_n, 8, nz), f32),
             pltpu.VMEM((8, nz), f32),
-            pltpu.VMEM((2, 16, 8, nz), f32),
-            pltpu.VMEM((2, 13, nx, nz), f32),
-            pltpu.VMEM((4, 16, nz), f32),
-            pltpu.VMEM((2, 16, 8, nz), f32),
-            pltpu.VMEM((2, 13, nx, nz), f32),
-            pltpu.VMEM((4, 16, nz), f32),
-            pltpu.SemaphoreType.DMA((8,)),
-            pltpu.SemaphoreType.DMA((8,)),
+            pltpu.VMEM((2, 2, 12, 8, nz), f32),
+            pltpu.VMEM((2, 2, 11, nx, nz), f32),
+            pltpu.VMEM((2, 4, 16, nz), f32),
+            pltpu.VMEM((2, 2, 12, 8, nz), f32),
+            pltpu.VMEM((2, 2, 11, nx, nz), f32),
+            pltpu.VMEM((2, 4, 16, nz), f32),
+            pltpu.SemaphoreType.DMA((2, 8)),
+            pltpu.SemaphoreType.DMA((2, 8)),
             pltpu.VMEM((2, blocks + 1, 8, nz), f32),
             pltpu.SemaphoreType.DMA((4,)),
             pltpu.SemaphoreType.DMA((STEPS, 8)),

time: 154 us -> 148 us (0.961)
  Pallas kernels: 142 us -> 136 us
    pallas_call x1, Pallas kernels: 142 us -> 136 us  [body(): pl.pallas_call(functools.partial(kernel, lon_n, lat_n), out_shape=(jax.Sh...]
where the time goes in v4:
time: 148 us; the launch traced here: 146 us
  Pallas kernels  136 us (92%)
  local copies, waits for them, and re-layouts  9.62 us (6%)
    pallas_call x1, Pallas kernels, body(): pl.pallas_call(functools.partial(kernel, lon_n, lat_n), out_shape=(jax.Sh...  136 us
    unnamed x10, local copies, waits for them, and re-layouts  6.32 us
    pallas_call x2, local copies, waits for them, and re-layouts, body(): pl.pallas_call(functools.partial(kernel, lon_n, lat_n), out_shape=(jax.Sh...  3.31 us

profile of v4, /device:TPU:1, one launch (start us, length us, event | category | flops | bytes accessed | tf_op | source)
XLA Modules:
  0.0 145.9 jit_solution(2294793014355466269)
XLA Ops:
  0.6 0.0 copy-start
  0.6 1.9 %copy.8.p_hbm = f32[16,12,384]{2,1,0:T(8,128)} copy(f32[16,12,384]{2,0,1:T(8,128)} %param.6) | data formatting | bytes 589824 | tf_op args[1]
  2.5 1.8 %copy.9.vis_hbm = f32[16,12,384]{2,1,0:T(8,128)} copy(f32[16,12,384]{2,0,1:T(8,128)} %param.7) | data formatting | bytes 589824 | tf_op args[2]
  4.3 0.0 copy-done
  4.3 0.0 copy-start.1
  4.3 1.3 copy.7.vel_hbm
  5.6 0.0 copy-done.1
  5.6 1.3 copy.10.force_hbm
  7.0 135.6 %vanka.1 = (f32[3,16,12,384]{3,2,1,0:T(8,128)}, f32[16,12,384]{2,1,0:T(8,128)}) custom-call(s32[8]{0:T(128)} %order_ref.1, f32[3,16,12,384]{3,2,1,0:T(8,128)} %copy.7.vel_hbm, f32[16,12,384]{2,1,0:T(8,128)} %copy.8.p_hbm, f32[16,12,384]{2,1,0:T(8,128)} %copy.9.vis_hbm, f32[3,16,12,384]{3,2,1,0:T(8,128)} %copy.10.force_hbm), custom_call_target="tpu_custom_call" | custom-call | tf_op jit(solution)/shard_map/vanka/pallas_call | solution.py:693
  142.6 0.0 copy-start.2
  142.6 2.5 %copy.11 = f32[3,16,12,384]{3,1,2,0:T(8,128)} copy(f32[3,16,12,384]{3,2,1,0:T(8,128)} %get-tuple-element.2) | data formatting | bytes 1769472 | tf_op jit(solution)/shard_map/vanka/pallas_call | solution.py:693
  145.1 0.0 copy-done.2
  145.1 0.8 copy.12
Async XLA Ops:
  0.6 3.7 %copy-start = (f32[3,16,12,384]{3,1,2,0:T(8,128)S(1)}, f32[3,16,12,384]{3,1,2,0:T(8,128)}, u32[]{:S(2)}) copy-start(f32[3,16,12,384]{3,1,2,0:T(8,128)} %param.5) | copy-start | bytes 2654212
  4.3 1.3 copy-start.1
  142.6 2.5 %copy-start.2 = (f32[16,12,384]{2,1,0:T(8,128)S(1)}, f32[16,12,384]{2,1,0:T(8,128)}, u32[]{:S(2)}) copy-start(f32[16,12,384]{2,1,0:T(8,128)} %get-tuple-element.3) | copy-start | bytes 884740

commit v5 on v4

--- a/solution.py
+++ b/solution.py
@@ -13,11 +13,12 @@
 STEPS = SWEEPS * COLOURS
 DAMP = 0.6
 GAIN = 0.25
+NEAR_ROWS, MID_ROWS = 24, 16
 SENT = 4
 NEW = 6
 FIRST = 16
 MESH = pl.DeviceIdType.MESH
-DIRECTIONS = ((1, 0), (-1, 0), (0, 1), (0, -1), (1, 1), (1, -1), (-1, 1), (-1, -1))
+DIRECTIONS = ((1, 0), (-1, 0), (0, 1), (0, -1), (1, 1), (1, -1), (-1, 1), (-1, -1), (0, 1), (0, -1))
 
 
 def opposite(n):
@@ -72,6 +73,8 @@
     first_recv_c,
     first_send_sem,
     first_recv_sem,
+    send_mid,
+    recv_mid,
     pack,
     load_sem,
     send_sem,
@@ -378,6 +381,8 @@
             src, dst = send_x.at[side, n], recv_x.at[side, n]
         elif n < 4:
             src, dst = send_y.at[side, n - 2], recv_y.at[side, n - 2]
+        elif n >= 8:
+            src, dst = send_mid.at[side, n - 8], recv_mid.at[side, n - 8]
         else:
             src, dst = send_c.at[side, n - 4], recv_c.at[side, n - 4]
         return pltpu.make_async_remote_copy(
@@ -389,7 +394,38 @@
             device_id_type=MESH,
         )
 
-    def sweep(s, table):
+    near = (1, 2, blocks - 2, blocks - 1, blocks)
+    mid = tuple(range(3, blocks - 2))
+
+    def margin_rows(side, which, way, row):
+        base = FIRST + NEW * side
+        z_parity = (order_ref[lax.rem(side, COLOURS)] >> 2) & 1
+        zrow = (lanes[0:1] & 1) == z_parity
+        buffer, group = (recv_y, near) if which == 0 else (recv_mid, mid)
+        per = len(group)
+        got = buffer[side, way]
+        turned = roll_lanes(got[0:16], -1)
+        for k, v, at, mixed in (
+            (0, got, 0, True),
+            (1, got, per, True),
+            (2, got, 2 * per, False),
+            (3, got, 3 * per, False),
+            (4, turned, per, True),
+            (5, turned, 0, True),
+        ):
+            for n, block in enumerate(group):
+                new_row = v[at + n : at + n + 1]
+                if mixed:
+                    new_row = jnp.where(zrow, new_row, slots[base + k, block + 1, row : row + 1])
+                slots[base + k, block + 1, row : row + 1] = new_row
+
+    def finish_mid(side):
+        for n in (8, 9):
+            guarded(present(opposite(n)), lambda n=n: copy(n, side).wait_recv())
+        pl.when(has_low)(lambda: margin_rows(side, 1, 0, 0))
+        pl.when(has_high)(lambda: margin_rows(side, 1, 1, 7))
+
+    def prepare(s, table):
         colour = order_ref[lax.rem(s, COLOURS)]
         a = colour & 1
         b = (colour >> 1) & 1
@@ -476,89 +512,101 @@
             slots[base + 5, block + 1] = new_x
             return carry
 
-        lax.fori_loop(0, 2, lambda n, t: block_step(1 + n * (blocks - 1), t), 0)
-
         def packed_tile(k, block):
             return pack.at[k, block] if k < 2 else slots.at[base + k, block + 1]
 
-        for k in range(SENT):
-            send_x[side, 0, k] = packed_tile(k, blocks)[...]
-            send_x[side, 1, k] = packed_tile(k, 1)[...]
-            for n in range(4):
-                dx, dy = DIRECTIONS[4 + n]
-                row = 6 if dy > 0 else 1
-                source = packed_tile(k, blocks if dx > 0 else 1)
-                send_c[side, n, k : k + 1] = source[row : row + 1]
-        for n in (4, 5, 6, 7, 0, 1):
-            guarded(present(n), lambda n=n: copy(n, side).start())
-        lax.fori_loop(2, blocks, block_step, 0, unroll=2)
-        for k in range(SENT):
-            for block in range(1, blocks + 1):
-                source = packed_tile(k, block)
-                send_y[side, 0, k, block - 1 : block] = source[6:7]
-                send_y[side, 1, k, block - 1 : block] = source[1:2]
-        for n in (2, 3):
-            guarded(present(n), lambda n=n: copy(n, side).start())
-        for n in range(8):
-            guarded(present(opposite(n)), lambda n=n: copy(n, side).wait_recv())
-
-        for way, at, low_c, high_c in ((0, 1, 0, 1), (1, blocks + 2, 2, 3)):
-            tiles = []
+        def edge():
+            lax.fori_loop(0, 2, lambda n, t: block_step(1 + n * (blocks - 1), t), 0)
+
             for k in range(SENT):
-                v = recv_x[side, way, k]
-                v = jnp.where((rows == 0) & has_low, recv_c[side, low_c, k : k + 1], v)
-                v = jnp.where((rows == 7) & has_high, recv_c[side, high_c, k : k + 1], v)
-                tiles.append(v)
-            x_index = jnp.minimum(at + a + shift[1, 0], blocks + 2)
-            slots[base + 0, at] = jnp.where(zmask, tiles[0], field(0, 0, 0, at - 1))
-            slots[base + 1, at] = jnp.where(zmask, tiles[1], field(1, 0, 0, at - 1))
-            slots[base + 2, at] = tiles[2]
-            slots[base + 3, at] = tiles[3]
-            slots[base + 4, at] = jnp.where(
-                zmask, roll_lanes(tiles[1], -1), field(1, 0, 1, at - 1)
-            )
-            slots[base + 5, at] = jnp.where(
-                zmask, roll_lanes(tiles[0], -1), slots[rel[0, 1, 0], x_index]
-            )
-
-        zrow = zmask[0:1]
-
-        def margin_rows(way, row):
-            got = [recv_y[side, way, k] for k in range(SENT)]
-            turned = [roll_lanes(got[0], -1), roll_lanes(got[1], -1)]
-            for k, v, mixed in (
-                (0, got[0], True),
-                (1, got[1], True),
-                (2, got[2], False),
-                (3, got[3], False),
-                (4, turned[1], True),
-                (5, turned[0], True),
-            ):
-                for block in range(1, blocks + 1):
-                    new_row = v[block - 1 : block]
-                    if mixed:
-                        new_row = jnp.where(zrow, new_row, slots[base + k, block + 1, row : row + 1])
-                    slots[base + k, block + 1, row : row + 1] = new_row
-
-        pl.when(has_low)(lambda: margin_rows(0, 0))
-        pl.when(has_high)(lambda: margin_rows(1, 7))
-
-        new = list(table)
-        for xp in (0, 1):
-            for yp in (0, 1):
-                at = xp * 2 + yp
-                same = (a == xp) & (b == yp)
-                x_next = (a != xp) & (b == yp)
-                y_next = (a == xp) & (b != yp)
-                new[at] = jnp.where(same, base, jnp.where(x_next, base + 5, table[at]))
-                new[16 + at] = jnp.where(same, 0, jnp.where(x_next, -a, table[16 + at]))
-                new[4 + at] = jnp.where(same, base + 1, jnp.where(y_next, base + 4, table[4 + at]))
-                new[8 + at] = jnp.where(same, base + 2, table[8 + at])
-                new[12 + at] = jnp.where(same, base + 3, table[12 + at])
-        return tuple(new)
+                send_x[side, 0, k] = packed_tile(k, blocks)[...]
+                send_x[side, 1, k] = packed_tile(k, 1)[...]
+                for n in range(4):
+                    dx, dy = DIRECTIONS[4 + n]
+                    row = 6 if dy > 0 else 1
+                    source = packed_tile(k, blocks if dx > 0 else 1)
+                    send_c[side, n, k : k + 1] = source[row : row + 1]
+            for n in (4, 5, 6, 7, 0, 1):
+                guarded(present(n), lambda n=n: copy(n, side).start())
+
+        def inner():
+            for block in (2, blocks - 2, blocks - 1):
+                block_step(block, 0)
+
+            def stage_rows(buffer, group):
+                for k in range(SENT):
+                    for n, block in enumerate(group):
+                        at = k * len(group) + n
+                        source = packed_tile(k, block)
+                        buffer[side, 0, at : at + 1] = source[6:7]
+                        buffer[side, 1, at : at + 1] = source[1:2]
+
+            stage_rows(send_y, near)
+            for n in (2, 3):
+                guarded(present(n), lambda n=n: copy(n, side).start())
+            lax.fori_loop(3, blocks - 2, block_step, 0)
+            stage_rows(send_mid, mid)
+            for n in (8, 9):
+                guarded(present(n), lambda n=n: copy(n, side).start())
+
+        def receive():
+            for n in range(8):
+                guarded(present(opposite(n)), lambda n=n: copy(n, side).wait_recv())
+
+            for way, at, low_c, high_c in ((0, 1, 0, 1), (1, blocks + 2, 2, 3)):
+                tiles = []
+                for k in range(SENT):
+                    v = recv_x[side, way, k]
+                    v = jnp.where((rows == 0) & has_low, recv_c[side, low_c, k : k + 1], v)
+                    v = jnp.where((rows == 7) & has_high, recv_c[side, high_c, k : k + 1], v)
+                    tiles.append(v)
+                x_index = jnp.minimum(at + a + shift[1, 0], blocks + 2)
+                slots[base + 0, at] = jnp.where(zmask, tiles[0], field(0, 0, 0, at - 1))
+                slots[base + 1, at] = jnp.where(zmask, tiles[1], field(1, 0, 0, at - 1))
+                slots[base + 2, at] = tiles[2]
+                slots[base + 3, at] = tiles[3]
+                slots[base + 4, at] = jnp.where(
+                    zmask, roll_lanes(tiles[1], -1), field(1, 0, 1, at - 1)
+                )
+                slots[base + 5, at] = jnp.where(
+                    zmask, roll_lanes(tiles[0], -1), slots[rel[0, 1, 0], x_index]
+                )
+
+            pl.when(has_low)(lambda: margin_rows(side, 0, 0, 0))
+            pl.when(has_high)(lambda: margin_rows(side, 0, 1, 7))
+
+            new = list(table)
+            for xp in (0, 1):
+                for yp in (0, 1):
+                    at = xp * 2 + yp
+                    same = (a == xp) & (b == yp)
+                    x_next = (a != xp) & (b == yp)
+                    y_next = (a == xp) & (b != yp)
+                    new[at] = jnp.where(same, base, jnp.where(x_next, base + 5, table[at]))
+                    new[16 + at] = jnp.where(same, 0, jnp.where(x_next, -a, table[16 + at]))
+                    new[4 + at] = jnp.where(same, base + 1, jnp.where(y_next, base + 4, table[4 + at]))
+                    new[8 + at] = jnp.where(same, base + 2, table[8 + at])
+                    new[12 + at] = jnp.where(same, base + 3, table[12 + at])
+            return tuple(new)
+
+        return edge, inner, receive
 
     table = tuple(jnp.int32(n) for n in range(16)) + tuple(jnp.int32(0) for _ in range(4))
-    table = lax.fori_loop(0, STEPS, sweep, table)
+    prepare(0, table)[0]()
+
+    def sweep(s, table):
+        _, inner, receive = prepare(s, table)
+        inner()
+        table = receive()
+        prepare(s + 1, table)[0]()
+        finish_mid(s)
+        return table
+
+    table = lax.fori_loop(0, STEPS - 1, sweep, table)
+    _, inner, receive = prepare(STEPS - 1, table)
+    inner()
+    table = receive()
+    finish_mid(STEPS - 1)
 
     def final(f, xp, yp, block):
         index = block + 1
@@ -637,7 +685,7 @@
             guarded(present(n), lambda p=part_no, n=n: first_copy(p, n).wait_send())
 
     def drain(s, carry):
-        for n in range(8):
+        for n in range(10):
             guarded(present(n), lambda n=n: copy(n, s).wait_send())
         return carry
 
@@ -712,10 +760,10 @@
             pltpu.VMEM((nx + 4, 2, 8, nz), f32),
             pltpu.VMEM((nx + 4, 2, 8, nz), f32),
             pltpu.VMEM((STEPS, 2, SENT, 8, nz), f32),
-            pltpu.VMEM((STEPS, 2, SENT, 8, nz), f32),
+            pltpu.VMEM((STEPS, 2, NEAR_ROWS, nz), f32),
             pltpu.VMEM((STEPS, 4, 8, nz), f32),
             pltpu.VMEM((STEPS, 2, SENT, 8, nz), f32),
-            pltpu.VMEM((STEPS, 2, SENT, 8, nz), f32),
+            pltpu.VMEM((STEPS, 2, NEAR_ROWS, nz), f32),
             pltpu.VMEM((STEPS, 4, 8, nz), f32),
             pltpu.VMEM((lon_n, 8, nz), f32),
             pltpu.VMEM((8, nz), f32),
@@ -727,10 +775,12 @@
             pltpu.VMEM((2, 4, 16, nz), f32),
             pltpu.SemaphoreType.DMA((2, 8)),
             pltpu.SemaphoreType.DMA((2, 8)),
+            pltpu.VMEM((STEPS, 2, MID_ROWS, nz), f32),
+            pltpu.VMEM((STEPS, 2, MID_ROWS, nz), f32),
             pltpu.VMEM((2, blocks + 1, 8, nz), f32),
             pltpu.SemaphoreType.DMA((4,)),
-            pltpu.SemaphoreType.DMA((STEPS, 8)),
-            pltpu.SemaphoreType.DMA((STEPS, 8)),
+            pltpu.SemaphoreType.DMA((STEPS, 10)),
+            pltpu.SemaphoreType.DMA((STEPS, 10)),
             pltpu.SemaphoreType.DMA((lon_n,)),
             pltpu.SemaphoreType.DMA((lon_n,)),
         ],

time: 148 us -> 141 us (0.953)
  Pallas kernels: 136 us -> 129 us
    pallas_call x1, Pallas kernels: 136 us -> 129 us  [body(): pl.pallas_call(functools.partial(kernel, lon_n, lat_n), out_shape=(jax.Sh...]
where the time goes in v5:
time: 141 us; the launch traced here: 140 us
  Pallas kernels  129 us (91%)
  local copies, waits for them, and re-layouts  9.62 us (7%)
    pallas_call x1, Pallas kernels, body(): pl.pallas_call(functools.partial(kernel, lon_n, lat_n), out_shape=(jax.Sh...  129 us
    unnamed x10, local copies, waits for them, and re-layouts  6.32 us
    pallas_call x2, local copies, waits for them, and re-layouts, body(): pl.pallas_call(functools.partial(kernel, lon_n, lat_n), out_shape=(jax.Sh...  3.31 us

profile of v5, /device:TPU:1, one launch (start us, length us, event | category | flops | bytes accessed | tf_op | source)
XLA Modules:
  0.0 139.8 jit_solution(12171623446578777843)
XLA Ops:
  0.6 0.0 copy-start
  0.6 1.9 %copy.8.p_hbm = f32[16,12,384]{2,1,0:T(8,128)} copy(f32[16,12,384]{2,0,1:T(8,128)} %param.6) | data formatting | bytes 589824 | tf_op args[1]
  2.5 1.8 %copy.9.vis_hbm = f32[16,12,384]{2,1,0:T(8,128)} copy(f32[16,12,384]{2,0,1:T(8,128)} %param.7) | data formatting | bytes 589824 | tf_op args[2]
  4.3 0.0 copy-done
  4.3 0.0 copy-start.1
  4.3 1.3 copy.7.vel_hbm
  5.6 0.0 copy-done.1
  5.6 1.3 copy.10.force_hbm
  7.0 129.5 %vanka.1 = (f32[3,16,12,384]{3,2,1,0:T(8,128)}, f32[16,12,384]{2,1,0:T(8,128)}) custom-call(s32[8]{0:T(128)} %order_ref.1, f32[3,16,12,384]{3,2,1,0:T(8,128)} %copy.7.vel_hbm, f32[16,12,384]{2,1,0:T(8,128)} %copy.8.p_hbm, f32[16,12,384]{2,1,0:T(8,128)} %copy.9.vis_hbm, f32[3,16,12,384]{3,2,1,0:T(8,128)} %copy.10.force_hbm), custom_call_target="tpu_custom_call" | custom-call | tf_op jit(solution)/shard_map/vanka/pallas_call | solution.py:741
  136.4 0.0 copy-start.2
  136.4 2.5 %copy.11 = f32[3,16,12,384]{3,1,2,0:T(8,128)} copy(f32[3,16,12,384]{3,2,1,0:T(8,128)} %get-tuple-element.2) | data formatting | bytes 1769472 | tf_op jit(solution)/shard_map/vanka/pallas_call | solution.py:741
  138.9 0.0 copy-done.2
  138.9 0.8 copy.12
Async XLA Ops:
  0.6 3.7 %copy-start = (f32[3,16,12,384]{3,1,2,0:T(8,128)S(1)}, f32[3,16,12,384]{3,1,2,0:T(8,128)}, u32[]{:S(2)}) copy-start(f32[3,16,12,384]{3,1,2,0:T(8,128)} %param.5) | copy-start | bytes 2654212
  4.3 1.3 copy-start.1
  136.4 2.5 %copy-start.2 = (f32[16,12,384]{2,1,0:T(8,128)S(1)}, f32[16,12,384]{2,1,0:T(8,128)}, u32[]{:S(2)}) copy-start(f32[16,12,384]{2,1,0:T(8,128)} %get-tuple-element.3) | copy-start | bytes 884740

commit v6 on v5

--- a/solution.py
+++ b/solution.py
@@ -516,7 +516,8 @@
             return pack.at[k, block] if k < 2 else slots.at[base + k, block + 1]
 
         def edge():
-            lax.fori_loop(0, 2, lambda n, t: block_step(1 + n * (blocks - 1), t), 0)
+            block_step(1, 0)
+            block_step(blocks, 0)
 
             for k in range(SENT):
                 send_x[side, 0, k] = packed_tile(k, blocks)[...]
@@ -544,7 +545,8 @@
             stage_rows(send_y, near)
             for n in (2, 3):
                 guarded(present(n), lambda n=n: copy(n, side).start())
-            lax.fori_loop(3, blocks - 2, block_step, 0)
+            for block in mid:
+                block_step(block, 0)
             stage_rows(send_mid, mid)
             for n in (8, 9):
                 guarded(present(n), lambda n=n: copy(n, side).start())

time: 141 us -> 140 us (level)
    pallas_call x1, Pallas kernels: 129 us -> 128 us  [body(): pl.pallas_call(functools.partial(kernel, lon_n, lat_n), out_shape=(jax.Sh...]
where the time goes in v6:
time: 140 us; the launch traced here: 138 us
  Pallas kernels  128 us (91%)
  local copies, waits for them, and re-layouts  9.62 us (7%)
    pallas_call x1, Pallas kernels, body(): pl.pallas_call(functools.partial(kernel, lon_n, lat_n), out_shape=(jax.Sh...  128 us
    unnamed x10, local copies, waits for them, and re-layouts  6.32 us
    pallas_call x2, local copies, waits for them, and re-layouts, body(): pl.pallas_call(functools.partial(kernel, lon_n, lat_n), out_shape=(jax.Sh...  3.31 us

profile of v6, /device:TPU:1, one launch (start us, length us, event | category | flops | bytes accessed | tf_op | source)
XLA Modules:
  0.0 138.2 jit_solution(1637996993077463095)
XLA Ops:
  0.6 0.0 copy-start
  0.6 1.9 %copy.8.p_hbm = f32[16,12,384]{2,1,0:T(8,128)} copy(f32[16,12,384]{2,0,1:T(8,128)} %param.6) | data formatting | bytes 589824 | tf_op args[1]
  2.5 1.8 %copy.9.vis_hbm = f32[16,12,384]{2,1,0:T(8,128)} copy(f32[16,12,384]{2,0,1:T(8,128)} %param.7) | data formatting | bytes 589824 | tf_op args[2]
  4.3 0.0 copy-done
  4.3 0.0 copy-start.1
  4.3 1.3 copy.7.vel_hbm
  5.6 0.0 copy-done.1
  5.6 1.3 copy.10.force_hbm
  7.0 127.9 %vanka.1 = (f32[3,16,12,384]{3,2,1,0:T(8,128)}, f32[16,12,384]{2,1,0:T(8,128)}) custom-call(s32[8]{0:T(128)} %order_ref.1, f32[3,16,12,384]{3,2,1,0:T(8,128)} %copy.7.vel_hbm, f32[16,12,384]{2,1,0:T(8,128)} %copy.8.p_hbm, f32[16,12,384]{2,1,0:T(8,128)} %copy.9.vis_hbm, f32[3,16,12,384]{3,2,1,0:T(8,128)} %copy.10.force_hbm), custom_call_target="tpu_custom_call" | custom-call | tf_op jit(solution)/shard_map/vanka/pallas_call | solution.py:743
  134.9 0.0 copy-start.2
  134.9 2.5 %copy.11 = f32[3,16,12,384]{3,1,2,0:T(8,128)} copy(f32[3,16,12,384]{3,2,1,0:T(8,128)} %get-tuple-element.2) | data formatting | bytes 1769472 | tf_op jit(solution)/shard_map/vanka/pallas_call | solution.py:743
  137.4 0.0 copy-done.2
  137.4 0.8 copy.12
Async XLA Ops:
  0.6 3.7 %copy-start = (f32[3,16,12,384]{3,1,2,0:T(8,128)S(1)}, f32[3,16,12,384]{3,1,2,0:T(8,128)}, u32[]{:S(2)}) copy-start(f32[3,16,12,384]{3,1,2,0:T(8,128)} %param.5) | copy-start | bytes 2654212
  4.3 1.3 copy-start.1
  134.9 2.5 %copy-start.2 = (f32[16,12,384]{2,1,0:T(8,128)S(1)}, f32[16,12,384]{2,1,0:T(8,128)}, u32[]{:S(2)}) copy-start(f32[16,12,384]{2,1,0:T(8,128)} %get-tuple-element.3) | copy-start | bytes 884740
